TPU v7x, 32 devices: a whole 2x2x4 slice. The times are simulated.
32 devices in a mesh: gz: 4 (over z), gy: 2 (over x), vec: 4 (over y, core).
Axes of the slice: x: 2, y: 2, z: 4, core: 2. Of those that a mesh axis runs over, the one named last changes fastest.
Arguments:
- vectors: bfloat16 [256, 3, 32, 4, 128], P('vec', None, 'gz', 'gy'), may hold values from -6 to 6
- links: bfloat16 [3, 3, 3, 32, 4, 128], P(None, None, None, 'gz', 'gy'), may hold values from -4 to 4
- momentum: int32 [3], replicated, may hold values from -5 to 5, as said below
- directions: int32 [3], replicated, may hold values from 0 to 2, each once
Outputs:
- elementals: float32 [4, 2, 256, 256], P(None, None, 'vec')
Inputs may be any that keep to these rules, and one draw needn't show every extreme that they name: `momentum`: one component is -5, another 5. `directions`: each of 0, 1, 2 once.
All inputs are finite; a program needn't handle non-finite values.
Results may differ from a plain program's by a relative error of at most 0.0029.
Values may be sent and summed in bfloat16 or wider, within the bound.
A program may use at most 128 MiB of HBM per device.

v0:
```python
import math

import jax
import jax.numpy as jnp
from jax import lax
from jax.sharding import PartitionSpec as P


def shifted(value, axis, steps):
    count = lax.axis_size(axis)
    pairs = [(source, (source + steps) % count) for source in range(count)]
    return lax.ppermute(value, axis, pairs)


def extended(block, sides, width):
    for axis, dim in sides:
        count = lax.axis_size(axis)
        forward = [(i, i + 1) for i in range(count - 1)]
        forward.append((count - 1, 0))
        backward = [(target, source) for source, target in forward]
        low = lax.ppermute(
            lax.slice_in_dim(block, block.shape[dim] - width, None, axis=dim), axis, forward
        )
        high = lax.ppermute(lax.slice_in_dim(block, 0, width, axis=dim), axis, backward)
        block = jnp.concatenate([low, block, high], axis=dim)
    return block


def apply_link(link_pair, field_pair):
    link_real, link_imag = link_pair
    field_real, field_imag = field_pair
    out_real = 0.0
    out_imag = 0.0
    for column in range(3):
        coeff_real = link_real[:, column][None]
        coeff_imag = link_imag[:, column][None]
        value_real = field_real[:, column][:, None]
        value_imag = field_imag[:, column][:, None]
        out_real = out_real + coeff_real * value_real - coeff_imag * value_imag
        out_imag = out_imag + coeff_real * value_imag + coeff_imag * value_real
    return (out_real, out_imag)


def apply_adjoint(link_pair, field_pair):
    link_real, link_imag = link_pair
    field_real, field_imag = field_pair
    out_real = 0.0
    out_imag = 0.0
    for column in range(3):
        coeff_real = link_real[column][None]
        coeff_imag = link_imag[column][None]
        value_real = field_real[:, column][:, None]
        value_imag = field_imag[:, column][:, None]
        out_real = out_real + coeff_real * value_real + coeff_imag * value_imag
        out_imag = out_imag + coeff_real * value_imag - coeff_imag * value_real
    return (out_real, out_imag)


def covariant(up_pair, down_pair, ahead_pair, behind_pair):
    forward = apply_link(up_pair, ahead_pair)
    backward = apply_adjoint(down_pair, behind_pair)
    return (0.5 * (forward[0] - backward[0]), 0.5 * (forward[1] - backward[1]))


def phase_table(momentum, x_coords, y_coords, z_coords, extent_x, extent_y, extent_z):
    frac_x = (momentum[0] * x_coords % extent_x).astype(jnp.float32) / extent_x
    frac_y = (momentum[1] * y_coords % extent_y).astype(jnp.float32) / extent_y
    frac_z = (momentum[2] * z_coords % extent_z).astype(jnp.float32) / extent_z
    summed = frac_z[:, None, None] + frac_y[None, :, None] + frac_x[None, None, :]
    angle = 2.0 * math.pi * summed
    return (jnp.cos(angle), jnp.sin(angle))


def make_operators(
    field_pair, ahead_list, behind_list, up_list, down_list, directions, cosine, sine
):
    derived = [
        covariant(
            up_list[axis_number],
            down_list[axis_number],
            ahead_list[axis_number],
            behind_list[axis_number],
        )
        for axis_number in range(3)
    ]
    results = []
    for op_slot in range(3):
        chosen = directions[op_slot]
        real_part = jnp.where(
            chosen == 0, derived[0][0], jnp.where(chosen == 1, derived[1][0], derived[2][0])
        )
        imag_part = jnp.where(
            chosen == 0, derived[0][1], jnp.where(chosen == 1, derived[1][1], derived[2][1])
        )
        results.append(jnp.stack([real_part, imag_part], -2).astype(jnp.bfloat16))
    field_real, field_imag = field_pair
    phased_real = field_real * cosine + field_imag * sine
    phased_imag = field_imag * cosine - field_real * sine
    results.append(jnp.stack([phased_real, phased_imag], -2).astype(jnp.bfloat16))
    return jnp.stack(results, 1)


def contract(rows, stacked_left):
    row_count = rows.shape[0]
    flat_rows = rows.reshape(row_count * 4, -1)
    product = lax.dot_general(
        flat_rows, stacked_left, (((1,), (1,)), ((), ())), preferred_element_type=jnp.float32
    )
    return product.reshape(row_count, 4, 2, stacked_left.shape[0] // 2)


def stack_left(six_dims):
    row_count = six_dims.shape[0]
    swapped = jnp.stack([-six_dims[..., 1, :], six_dims[..., 0, :]], -2)
    return jnp.concatenate([six_dims.reshape(row_count, -1), swapped.reshape(row_count, -1)], 0)


def link_parts(link_six):
    widened = link_six.astype(jnp.float32)
    return (widened[..., 0, :], widened[..., 1, :])


def stencil_lists(padded, row_count, slab_depth, height, width):
    widened = padded.astype(jnp.float32).reshape(row_count, 3, slab_depth + 2, height + 2, 2, width)
    pad_real = widened[..., 0, :]
    pad_imag = widened[..., 1, :]
    centre_real = pad_real[:, :, 1:-1, 1:-1]
    centre_imag = pad_imag[:, :, 1:-1, 1:-1]
    ahead_list = [
        (jnp.roll(centre_real, -1, axis=-1), jnp.roll(centre_imag, -1, axis=-1)),
        (pad_real[:, :, 1:-1, 2:], pad_imag[:, :, 1:-1, 2:]),
        (pad_real[:, :, 2:, 1:-1], pad_imag[:, :, 2:, 1:-1]),
    ]
    behind_list = [
        (jnp.roll(centre_real, 1, axis=-1), jnp.roll(centre_imag, 1, axis=-1)),
        (pad_real[:, :, 1:-1, :-2], pad_imag[:, :, 1:-1, :-2]),
        (pad_real[:, :, :-2, 1:-1], pad_imag[:, :, :-2, 1:-1]),
    ]
    return ((centre_real, centre_imag), ahead_list, behind_list)


def body(vectors, links, momentum, directions):
    local_count = vectors.shape[0]
    depth = vectors.shape[2]
    height = vectors.shape[3]
    width = vectors.shape[4] // 2
    links_six = links.reshape(3, 3, 3, depth, height, 2, width)
    x_down = jnp.roll(links_six[0], 1, axis=-1)
    y_link = links_six[1]
    y_rim = shifted(y_link[:, :, :, -1:], "gy", 1)
    y_down = jnp.concatenate([y_rim, y_link[:, :, :, :-1]], 3)
    z_link = links_six[2]
    z_rim = shifted(z_link[:, :, -1:], "gz", 1)
    z_down = jnp.concatenate([z_rim, z_link[:, :, :-1]], 2)
    up_six = [links_six[0], y_link, z_link]
    down_six = [x_down, y_down, z_down]
    extent_y = height * lax.axis_size("gy")
    extent_z = depth * lax.axis_size("gz")
    y_coords = lax.axis_index("gy") * height + jnp.arange(height, dtype=jnp.int32)
    z_coords = lax.axis_index("gz") * depth + jnp.arange(depth, dtype=jnp.int32)
    vec_parts = lax.axis_size("vec")
    all_vectors = local_count * vec_parts
    slab_depth = depth // vec_parts
    z_start = lax.axis_index("vec") * slab_depth
    pieces = vectors.reshape(local_count, 3, vec_parts, slab_depth, height, 2 * width)
    regrouped = lax.all_to_all(pieces, "vec", split_axis=2, concat_axis=0, tiled=True).reshape(
        all_vectors, 3, slab_depth, height, 2 * width
    )
    padded = extended(regrouped, ((("gz", "vec"), 2), ("gy", 3)), 1)
    centre, ahead_list, behind_list = stencil_lists(padded, all_vectors, slab_depth, height, width)
    up_list = [
        link_parts(lax.dynamic_slice_in_dim(link_six, z_start, slab_depth, 2))
        for link_six in up_six
    ]
    down_list = [
        link_parts(lax.dynamic_slice_in_dim(link_six, z_start, slab_depth, 2))
        for link_six in down_six
    ]
    slab_coords = lax.dynamic_slice_in_dim(z_coords, z_start, slab_depth, 0)
    cosine, sine = phase_table(
        momentum,
        jnp.arange(width, dtype=jnp.int32),
        y_coords,
        slab_coords,
        width,
        extent_y,
        extent_z,
    )
    transformed = make_operators(
        centre, ahead_list, behind_list, up_list, down_list, directions, cosine, sine
    )
    transformed_rows = transformed.reshape(all_vectors, 4, -1)
    stacked_left = stack_left(regrouped.reshape(all_vectors, 3, slab_depth, height, 2, width))
    partial_sums = lax.psum_scatter(
        contract(transformed_rows, stacked_left), "vec", scatter_dimension=0, tiled=True
    )
    summed = lax.psum(partial_sums, ("gz", "gy"))
    scaled = summed * (1.0 / math.sqrt(width * extent_y * extent_z))
    return jnp.transpose(scaled, (1, 2, 0, 3))


def solution(mesh):
    in_specs = (P("vec", None, "gz", "gy", None), P(None, None, None, "gz", "gy", None), P(), P())
    out_specs = P(None, None, "vec", None)
    return jax.shard_map(body, mesh=mesh, in_specs=in_specs, out_specs=out_specs, check_vma=False)
```

profile of v0, /device:TPU:0, one launch (start us, length us, event | category | flops | bytes accessed | tf_op | source)
XLA Modules:
  0.0 334.3 jit_solution(7995214610599245555)
XLA Ops:
  7.5 3.1 collective-permute-start.5
  12.4 2.2 copy.140
  14.7 3.6 %all-to-all-start = ((bf16[64,3,4,2,2,128]{5,0,4,3,1,2:T(8,128)(2,1)}), bf16[64,3,4,2,2,128]{5,0,4,3,1,2:T(8,128)(2,1)S(1)}, u32[]{:S(2)}, u32[]{:S(2)}) async-start(bf16[64,3,4,2,2,128]{5,0,4,3,1,2:T(8,128)(2,1)} %copy.140), calls=%async_computation | async-start | bytes 1572864 | tf_op jit(solution)/shard_map/all_to_all | solution.py:166
  32.0 4.0 %collective-permute-start.1 = (bf16[256,3,1,2,128]{4,0,3,2,1:T(8,128)(2,1)S(1)}, bf16[256,3,1,2,128]{4,0,3,2,1:T(8,128)(2,1)S(1)}, u32[]{:S(2)}, u32[]{:S(2)}) collective-permute-start(bf16[256,3,1,2,128]{4,0,3,2,1:T(8,128)(2,1)S(1)} %get-tuple-element.70), channel_id=1, source_target_pairs={{1,0},{2,1},{3,2},{8,3},{9,8},{10,9},{11,10},{16,11},{17,16},{18,1... | collective-permute-start | bytes 1179656 | tf_op jit(solution)/shard_map/ppermute | solution.py:24
  38.0 3.8 %collective-permute-done = bf16[256,3,1,2,128]{4,0,3,2,1:T(8,128)(2,1)S(1)} collective-permute-done((bf16[256,3,1,2,128]{4,0,3,2,1:T(8,128)(2,1)}, bf16[256,3,1,2,128]{4,0,3,2,1:T(8,128)(2,1)S(1)}, u32[]{:S(2)}, u32[]{:S(2)}) %collective-permute-start) | collective-permute-done | bytes 393248 | tf_op jit(solution)/shard_map/ppermute | solution.py:21
  45.9 4.5 %slice_negate_fusion = (bf16[256,3,2,2,1,64]{5,4,0,3,2,1:T(2,128)(2,1)}, bf16[256,3,2,2,1,64]{5,4,0,3,2,1:T(2,128)(2,1)}) fusion(bf16[256,3,2,2,2,64]{5,4,0,3,2,1:T(2,128)(2,1)S(1)} %concatenate.67), kind=kLoop, calls=%fused_computation.9 | loop fusion | flops 196608 | bytes 1572864 | tf_op jit(solution)/shard_map/neg | solution.py:114
  52.4 5.4 %pad_maximum_fusion.2 = bf16[256,3,2,2,2,64]{5,4,0,3,2,1:T(2,128)(2,1)S(1)} fusion(bf16[256,3,2,2,1,64]{5,4,0,3,2,1:T(2,128)(2,1)} %get-tuple-element.64, bf16[256,3,2,2,1,64]{5,4,0,3,2,1:T(2,128)(2,1)} %get-tuple-element.63), kind=kLoop, calls=%fused_computation.12 | loop fusion | flops 1572864 | bytes 1572864 | tf_op jit(solution)/shard_map/stack | solution.py:114
  57.8 2.6 copy.203
  67.1 2.3 copy.142
  69.4 3.5 %copy.148 = bf16[256,3,4,1,2,64]{5,4,0,3,2,1:T(2,128)(2,1)S(1)} copy(bf16[256,3,4,1,2,64]{0,5,4,2,1,3:T(8,128)(2,1)} %bitcast.223) | data formatting | bytes 1572864 | tf_op jit(solution)/shard_map/concatenate | solution.py:25
  72.9 6.3 %collective-permute-done.3 = bf16[256,3,4,1,128]{4,0,3,2,1:T(8,128)(2,1)} collective-permute-done((bf16[256,3,4,1,128]{4,0,3,2,1:T(8,128)(2,1)}, bf16[256,3,4,1,128]{4,0,3,2,1:T(8,128)(2,1)}, u32[]{:S(2)}, u32[]{:S(2)}) %collective-permute-start.3) | collective-permute-done | bytes 786464 | tf_op jit(solution)/shard_map/ppermute | solution.py:24
  79.2 2.3 copy.147
  81.5 4.8 %copy.149 = bf16[256,3,4,1,2,64]{5,4,0,3,2,1:T(2,128)(2,1)} copy(bf16[256,3,4,1,2,64]{0,5,4,2,1,3:T(8,128)(2,1)} %bitcast.224) | data formatting | bytes 1572864 | tf_op jit(solution)/shard_map/concatenate | solution.py:25
  86.3 12.6 %maximum_convert_fusion = f32[256,3,4,4,2,64]{5,4,0,3,2,1:T(2,128)S(1)} fusion(bf16[256,3,4,1,2,64]{5,4,0,3,2,1:T(2,128)(2,1)} %copy.149, bf16[256,3,1,2,2,64]{5,4,0,3,2,1:T(2,128)(2,1)} %copy.146, bf16[256,3,2,2,2,64]{5,4,0,3,2,1:T(2,128)(2,1)S(1)} %concatenate.67, bf16[256,3,1,2,2,64]{5,4,0,3,2,1:T(2,128)(2,1)} %copy.145, ...), kind=kLoop, calls=%fused_computation | loop fusion | flops 7864320 | bytes 9437184 | tf_op jit(solution)/shard_map/convert_element_type | solution.py:124
  98.9 10.1 %fusion.47 = (f32[256,3,4,4,1,64]{5,4,0,3,2,1:T(1,128)S(1)}, f32[256,3,4,4,1,64]{5,4,0,3,2,1:T(1,128)S(1)}) fusion(f32[256,3,4,4,2,64]{5,4,0,3,2,1:T(2,128)S(1)} %maximum_convert_fusion), kind=kLoop, calls=%fused_computation.183 | loop fusion | bytes 12582912 | tf_op jit(solution)/shard_map/slice | solution.py:126
  111.7 3.2 slice_bitcast_fusion.23
  115.4 2.2 fusion.48
  117.6 2.7 slice_bitcast_fusion.22
  120.3 2.5 fusion.16
  124.0 1.9 copy.166
  125.9 1.9 copy.193
  129.7 1.9 copy.189
  131.7 1.9 copy.185
  133.6 1.9 copy.183
  135.5 1.9 copy.181
  137.5 1.9 copy.178
  139.4 1.9 copy.176
  141.3 1.9 copy.174
  143.2 1.9 copy.170
  145.2 1.9 copy.168
  147.1 1.9 copy.163
  149.0 1.9 copy.161
  151.0 1.9 copy.153
  152.9 1.9 copy.155
  154.8 1.9 copy.151
  156.7 4.4 %fusion.12 = (f32[256,2,2,64]{3,0,2,1:T(8,128)}, f32[256,2,2,64]{3,0,2,1:T(8,128)}, f32[256,2,2,64]{3,0,2,1:T(8,128)}, f32[256,2,2,64]{3,0,2,1:T(8,128)}, f32[25...) fusion(f32[256,3,2,2,1]{4,0,3,2,1:T(8,128)S(1)} %get-tuple-element.20, f32[256,3,2,2,63]{4,0,3,2,1:T(8,128)} %get-tuple-element.18, ...), kind=kLoop, calls=%fused_computation.52 | loop fusion | flops 393216 | bytes 3145728 | tf_op jit(solution)/shard_map/mul | solution.py:54
  161.1 2.1 copy.160
  163.2 2.0 copy.167
  176.0 2.1 copy.162
  178.1 1.9 copy.154
  180.1 1.9 copy.156
  182.0 1.9 copy.152
  184.3 9.4 %select_convert_fusion.4 = (bf16[256,1,3,2,2,1,64]{0,6,5,4,3,2,1:T(8,128)(2,1)}, bf16[256,1,3,2,2,1,64]{0,6,5,4,3,2,1:T(8,128)(2,1)}, bf16[256,1,3,2,2,1,64]{0,6...) fusion(pred[]{:T(512)} %bitcast.39, pred[]{:T(512)} %bitcast, f32[256,2,2,64]{0,3,2,1:T(8,128)S(1)} %copy-done.4, ...), kind=kLoop, calls=%fused_computation.41 | loop fusion | flops 15138816 | bytes 11120642 | tf_op jit(solution)/shard_map/convert.9
  194.0 7.9 %select_convert_fusion.5 = (bf16[256,1,3,2,2,1,64]{0,6,5,4,3,2,1:T(8,128)(2,1)}, bf16[256,1,3,2,2,1,64]{0,6,5,4,3,2,1:T(8,128)(2,1)}, bf16[256,1,3,2,2,1,64]{0,6...) fusion(pred[]{:T(512)} %bitcast.39, pred[]{:T(512)} %bitcast, f32[256,2,2,64]{0,3,2,1:T(8,128)S(1)} %copy-done.22, ...), kind=kLoop, calls=%fused_computation.45 | loop fusion | flops 15138816 | bytes 11120642 | tf_op jit(solution)/shard_map/convert.8
  201.9 2.3 fusion.7
  211.6 4.7 %fusion = f32[256,4,2,256]{3,0,2,1:T(8,128)} fusion(bf16[2,256,1536,1]{2,1,0,3:T(8,128)(2,1)S(1)} %bitcast.226, bf16[256,1,1536]{2,0,1:T(8,128)(2,1)S(1)} %copy-done.61, bf16[256,1,1536]{2,0,1:T(8,128)(2,1)} %copy.200, bf16[256,1,1536]{2,0,1:T(8,128)(2,1)} %copy.199, bf16[256,1,1536]{2,0,1:T(8,128)(2,1)} %copy.198), kind=kOutput, calls=%fused_computation.2 | convolution fusion | flops 1623195648 | bytes 6815744 | tf_op jit(solution)/shard_map/dot_general | solution.py:106
  216.4 33.0 %reduce-scatter.2.cloned.1.call-done = f32[64,4,2,256]{3,0,2,1:T(8,128)} async-done(((f32[256,4,2,256]{3,0,2,1:T(8,128)}), f32[64,4,2,256]{3,0,2,1:T(8,128)}) %reduce-scatter.2.cloned.1.call-update) | async-done | bytes 524304 | tf_op jit(solution)/shard_map/reduce_scatter | solution.py:194
  249.4 76.2 %all-reduce.2.cloned.1.call-done = f32[64,4,2,256]{3,0,2,1:T(8,128)} async-done(((f32[64,4,2,256]{3,0,2,1:T(8,128)}), f32[64,4,2,256]{3,0,2,1:T(8,128)}) %all-reduce.2.cloned.1.call-update) | async-done | bytes 524304 | tf_op jit(solution)/shard_map/psum | solution.py:197
  (228 shorter events, 53.7 us)
Async XLA Ops:
  7.5 22.4 %collective-permute-start.5 = (bf16[3,3,1,2,2,64]{5,3,2,1,4,0:T(2,128)(2,1)S(1)}, bf16[3,3,1,2,2,64]{5,3,2,1,4,0:T(2,128)(2,1)S(1)}, u32[]{:S(2)}, u32[]{:S(2)}) collective-permute-start(bf16[3,3,1,2,2,64]{5,3,2,1,4,0:T(2,128)(2,1)S(1)} %copy.217), channel_id=1, source_target_pairs={{0,8},{8,16},{16,24},{24,0},{1,9},{9,17},{17,25},{25,1},{2,10},{10... | collective-permute-start | bytes 13832 | tf_op jit(solution)/shard_map/ppermute | solution.py:12
  10.9 19.8 %collective-permute-start.4 = (bf16[3,3,8,1,2,64]{5,3,2,1,4,0:T(2,128)(2,1)S(1)}, bf16[3,3,8,1,2,64]{5,3,2,1,4,0:T(2,128)(2,1)S(1)}, u32[]{:S(2)}, u32[]{:S(2)}) collective-permute-start(bf16[3,3,8,1,2,64]{5,3,2,1,4,0:T(2,128)(2,1)S(1)} %copy.214), channel_id=1, source_target_pairs={{0,4},{4,0},{1,5},{5,1},{2,6},{6,2},{3,7},{7,3},{8,12},{12,8},{9,1... | collective-permute-start | bytes 55304 | tf_op jit(solution)/shard_map/ppermute | solution.py:12
  14.6 10.5 %copy-start.66 = (s32[3]{0:T(128)S(1)}, s32[3]{0:T(128)}, u32[]{:S(2)}) copy-start(s32[3]{0:T(128)} %param.7) | copy-start | bytes 40
  14.7 16.1 %all-to-all-start = ((bf16[64,3,4,2,2,128]{5,0,4,3,1,2:T(8,128)(2,1)}), bf16[64,3,4,2,2,128]{5,0,4,3,1,2:T(8,128)(2,1)S(1)}, u32[]{:S(2)}, u32[]{:S(2)}) async-start(bf16[64,3,4,2,2,128]{5,0,4,3,1,2:T(8,128)(2,1)} %copy.140), calls=%async_computation | async-start | bytes 1572864 | tf_op jit(solution)/shard_map/all_to_all | solution.py:166
  18.3 231.1 %reduce-scatter.2.cloned.1.call-start = ((), (), s32[]{:S(2)}) async-start(), calls=%async_computation.2 | async-start | bytes 2621440 | tf_op jit(solution)/shard_map/reduce_scatter | solution.py:194
  31.6 10.2 %collective-permute-start = (bf16[256,3,1,2,128]{4,0,3,2,1:T(8,128)(2,1)}, bf16[256,3,1,2,128]{4,0,3,2,1:T(8,128)(2,1)S(1)}, u32[]{:S(2)}, u32[]{:S(2)}) collective-permute-start(bf16[256,3,1,2,128]{4,0,3,2,1:T(8,128)(2,1)} %get-tuple-element.69), channel_id=1, source_target_pairs={{0,1},{1,2},{2,3},{3,8},{8,9},{9,10},{10,11},{11,16},{16,17},{17,1... | collective-permute-start | bytes 1179656 | tf_op jit(solution)/shard_map/ppermute | solution.py:21
  32.0 9.8 %collective-permute-start.1 = (bf16[256,3,1,2,128]{4,0,3,2,1:T(8,128)(2,1)S(1)}, bf16[256,3,1,2,128]{4,0,3,2,1:T(8,128)(2,1)S(1)}, u32[]{:S(2)}, u32[]{:S(2)}) collective-permute-start(bf16[256,3,1,2,128]{4,0,3,2,1:T(8,128)(2,1)S(1)} %get-tuple-element.70), channel_id=1, source_target_pairs={{1,0},{2,1},{3,2},{8,3},{9,8},{10,9},{11,10},{16,11},{17,16},{18,1... | collective-permute-start | bytes 1179656 | tf_op jit(solution)/shard_map/ppermute | solution.py:24
  43.9 23.2 %collective-permute-start.2 = (bf16[256,3,4,1,128]{4,0,3,2,1:T(8,128)(2,1)}, bf16[256,3,4,1,128]{4,0,3,2,1:T(8,128)(2,1)}, u32[]{:S(2)}, u32[]{:S(2)}) collective-permute-start(bf16[256,3,4,1,128]{4,0,3,2,1:T(8,128)(2,1)} %get-tuple-element.61), channel_id=1, source_target_pairs={{0,4},{4,0},{1,5},{5,1},{2,6},{6,2},{3,7},{7,3},{8,12},{12,8},{9,1... | collective-permute-start | bytes 2359304 | tf_op jit(solution)/shard_map/ppermute | solution.py:21
  44.4 34.8 %collective-permute-start.3 = (bf16[256,3,4,1,128]{4,0,3,2,1:T(8,128)(2,1)}, bf16[256,3,4,1,128]{4,0,3,2,1:T(8,128)(2,1)}, u32[]{:S(2)}, u32[]{:S(2)}) collective-permute-start(bf16[256,3,4,1,128]{4,0,3,2,1:T(8,128)(2,1)} %get-tuple-element.62), channel_id=1, source_target_pairs={{4,0},{0,4},{5,1},{1,5},{6,2},{2,6},{7,3},{3,7},{12,8},{8,12},{13,... | collective-permute-start | bytes 2359304 | tf_op jit(solution)/shard_map/ppermute | solution.py:24
  109.0 8.6 %copy-start = (f32[256,3,4,4,1,64]{5,4,0,3,2,1:T(1,128)}, f32[256,3,4,4,1,64]{5,4,0,3,2,1:T(1,128)S(1)}, u32[]{:S(2)}) copy-start(f32[256,3,4,4,1,64]{5,4,0,3,2,1:T(1,128)S(1)} %get-tuple-element.15) | copy-start | bytes 9437188
  175.9 8.0 %copy-start.4 = (f32[256,2,2,64]{0,3,2,1:T(8,128)S(1)}, f32[256,2,2,64]{0,3,2,1:T(8,128)}, u32[]{:S(2)}) copy-start(f32[256,2,2,64]{0,3,2,1:T(8,128)} %copy.193) | copy-start | bytes 786436
  175.9 8.0 %copy-start.5 = (f32[256,2,2,64]{0,3,2,1:T(8,128)S(1)}, f32[256,2,2,64]{0,3,2,1:T(8,128)}, u32[]{:S(2)}) copy-start(f32[256,2,2,64]{0,3,2,1:T(8,128)} %copy.191) | copy-start | bytes 786436
  175.9 8.0 %copy-start.6 = (f32[256,2,2,64]{0,3,2,1:T(8,128)S(1)}, f32[256,2,2,64]{0,3,2,1:T(8,128)}, u32[]{:S(2)}) copy-start(f32[256,2,2,64]{0,3,2,1:T(8,128)} %copy.189) | copy-start | bytes 786436
  175.9 8.0 %copy-start.7 = (f32[256,2,2,64]{0,3,2,1:T(8,128)S(1)}, f32[256,2,2,64]{0,3,2,1:T(8,128)}, u32[]{:S(2)}) copy-start(f32[256,2,2,64]{0,3,2,1:T(8,128)} %copy.185) | copy-start | bytes 786436
  175.9 8.0 %copy-start.8 = (f32[256,2,2,64]{0,3,2,1:T(8,128)S(1)}, f32[256,2,2,64]{0,3,2,1:T(8,128)}, u32[]{:S(2)}) copy-start(f32[256,2,2,64]{0,3,2,1:T(8,128)} %copy.183) | copy-start | bytes 786436
  176.0 8.0 %copy-start.9 = (f32[256,2,2,64]{0,3,2,1:T(8,128)S(1)}, f32[256,2,2,64]{0,3,2,1:T(8,128)}, u32[]{:S(2)}) copy-start(f32[256,2,2,64]{0,3,2,1:T(8,128)} %copy.181) | copy-start | bytes 786436
  176.0 8.0 %copy-start.10 = (f32[256,2,2,64]{0,3,2,1:T(8,128)S(1)}, f32[256,2,2,64]{0,3,2,1:T(8,128)}, u32[]{:S(2)}) copy-start(f32[256,2,2,64]{0,3,2,1:T(8,128)} %copy.178) | copy-start | bytes 786436
  176.0 8.0 %copy-start.11 = (f32[256,2,2,64]{0,3,2,1:T(8,128)S(1)}, f32[256,2,2,64]{0,3,2,1:T(8,128)}, u32[]{:S(2)}) copy-start(f32[256,2,2,64]{0,3,2,1:T(8,128)} %copy.176) | copy-start | bytes 786436
  176.0 8.0 %copy-start.12 = (f32[256,2,2,64]{0,3,2,1:T(8,128)S(1)}, f32[256,2,2,64]{0,3,2,1:T(8,128)}, u32[]{:S(2)}) copy-start(f32[256,2,2,64]{0,3,2,1:T(8,128)} %copy.174) | copy-start | bytes 786436
  176.0 8.0 %copy-start.13 = (f32[256,2,2,64]{0,3,2,1:T(8,128)S(1)}, f32[256,2,2,64]{0,3,2,1:T(8,128)}, u32[]{:S(2)}) copy-start(f32[256,2,2,64]{0,3,2,1:T(8,128)} %copy.170) | copy-start | bytes 786436
  176.0 8.0 %copy-start.14 = (f32[256,2,2,64]{0,3,2,1:T(8,128)S(1)}, f32[256,2,2,64]{0,3,2,1:T(8,128)}, u32[]{:S(2)}) copy-start(f32[256,2,2,64]{0,3,2,1:T(8,128)} %copy.168) | copy-start | bytes 786436
  176.0 8.0 %copy-start.62 = (f32[3,2,2,64]{3,2,1,0:T(2,128)S(1)}, f32[3,2,2,64]{3,2,1,0:T(2,128)}, u32[]{:S(2)}) copy-start(f32[3,2,2,64]{3,2,1,0:T(2,128)} %get-tuple-element.110) | copy-start | bytes 9220
  176.0 8.0 %copy-start.63 = (f32[3,2,2,64]{3,2,1,0:T(2,128)S(1)}, f32[3,2,2,64]{3,2,1,0:T(2,128)}, u32[]{:S(2)}) copy-start(f32[3,2,2,64]{3,2,1,0:T(2,128)} %get-tuple-element.111) | copy-start | bytes 9220
  176.0 8.0 %copy-start.64 = (f32[3,2,2,64]{3,2,1,0:T(2,128)S(1)}, f32[3,2,2,64]{3,2,1,0:T(2,128)}, u32[]{:S(2)}) copy-start(f32[3,2,2,64]{3,2,1,0:T(2,128)} %get-tuple-element.112) | copy-start | bytes 9220
  184.1 9.7 %copy-start.15 = (f32[256,2,2,64]{0,3,2,1:T(8,128)S(1)}, f32[256,2,2,64]{0,3,2,1:T(8,128)}, u32[]{:S(2)}) copy-start(f32[256,2,2,64]{0,3,2,1:T(8,128)} %copy.163) | copy-start | bytes 786436
  184.1 9.7 %copy-start.16 = (f32[256,2,2,64]{0,3,2,1:T(8,128)S(1)}, f32[256,2,2,64]{0,3,2,1:T(8,128)}, u32[]{:S(2)}) copy-start(f32[256,2,2,64]{0,3,2,1:T(8,128)} %copy.161) | copy-start | bytes 786436
  184.1 9.7 %copy-start.17 = (f32[256,2,2,64]{0,3,2,1:T(8,128)S(1)}, f32[256,2,2,64]{0,3,2,1:T(8,128)}, u32[]{:S(2)}) copy-start(f32[256,2,2,64]{0,3,2,1:T(8,128)} %copy.153) | copy-start | bytes 786436
  184.1 9.7 %copy-start.18 = (f32[256,2,2,64]{0,3,2,1:T(8,128)S(1)}, f32[256,2,2,64]{0,3,2,1:T(8,128)}, u32[]{:S(2)}) copy-start(f32[256,2,2,64]{0,3,2,1:T(8,128)} %copy.155) | copy-start | bytes 786436
  184.1 9.7 %copy-start.19 = (f32[256,2,2,64]{0,3,2,1:T(8,128)S(1)}, f32[256,2,2,64]{0,3,2,1:T(8,128)}, u32[]{:S(2)}) copy-start(f32[256,2,2,64]{0,3,2,1:T(8,128)} %copy.151) | copy-start | bytes 786436
  184.1 9.7 %copy-start.20 = (f32[256,2,2,64]{0,3,2,1:T(8,128)S(1)}, f32[256,2,2,64]{0,3,2,1:T(8,128)}, u32[]{:S(2)}) copy-start(f32[256,2,2,64]{0,3,2,1:T(8,128)} %copy.160) | copy-start | bytes 786436
  184.1 9.7 %copy-start.21 = (f32[256,2,2,64]{0,3,2,1:T(8,128)S(1)}, f32[256,2,2,64]{0,3,2,1:T(8,128)}, u32[]{:S(2)}) copy-start(f32[256,2,2,64]{0,3,2,1:T(8,128)} %copy.167) | copy-start | bytes 786436
  184.1 9.7 %copy-start.22 = (f32[256,2,2,64]{0,3,2,1:T(8,128)S(1)}, f32[256,2,2,64]{0,3,2,1:T(8,128)}, u32[]{:S(2)}) copy-start(f32[256,2,2,64]{0,3,2,1:T(8,128)} %copy.194) | copy-start | bytes 786436
  184.2 9.7 %copy-start.23 = (f32[256,2,2,64]{0,3,2,1:T(8,128)S(1)}, f32[256,2,2,64]{0,3,2,1:T(8,128)}, u32[]{:S(2)}) copy-start(f32[256,2,2,64]{0,3,2,1:T(8,128)} %copy.192) | copy-start | bytes 786436
  184.2 9.7 %copy-start.24 = (f32[256,2,2,64]{0,3,2,1:T(8,128)S(1)}, f32[256,2,2,64]{0,3,2,1:T(8,128)}, u32[]{:S(2)}) copy-start(f32[256,2,2,64]{0,3,2,1:T(8,128)} %copy.190) | copy-start | bytes 786436
  184.2 9.7 %copy-start.25 = (f32[256,2,2,64]{0,3,2,1:T(8,128)S(1)}, f32[256,2,2,64]{0,3,2,1:T(8,128)}, u32[]{:S(2)}) copy-start(f32[256,2,2,64]{0,3,2,1:T(8,128)} %copy.186) | copy-start | bytes 786436
  184.2 9.7 %copy-start.26 = (f32[256,2,2,64]{0,3,2,1:T(8,128)S(1)}, f32[256,2,2,64]{0,3,2,1:T(8,128)}, u32[]{:S(2)}) copy-start(f32[256,2,2,64]{0,3,2,1:T(8,128)} %copy.184) | copy-start | bytes 786436
  184.2 9.7 %copy-start.27 = (f32[256,2,2,64]{0,3,2,1:T(8,128)S(1)}, f32[256,2,2,64]{0,3,2,1:T(8,128)}, u32[]{:S(2)}) copy-start(f32[256,2,2,64]{0,3,2,1:T(8,128)} %copy.182) | copy-start | bytes 786436
  184.2 9.7 %copy-start.28 = (f32[256,2,2,64]{0,3,2,1:T(8,128)S(1)}, f32[256,2,2,64]{0,3,2,1:T(8,128)}, u32[]{:S(2)}) copy-start(f32[256,2,2,64]{0,3,2,1:T(8,128)} %copy.179) | copy-start | bytes 786436
  184.2 9.7 %copy-start.29 = (f32[256,2,2,64]{0,3,2,1:T(8,128)S(1)}, f32[256,2,2,64]{0,3,2,1:T(8,128)}, u32[]{:S(2)}) copy-start(f32[256,2,2,64]{0,3,2,1:T(8,128)} %copy.177) | copy-start | bytes 786436
  184.2 9.7 %copy-start.30 = (f32[256,2,2,64]{0,3,2,1:T(8,128)S(1)}, f32[256,2,2,64]{0,3,2,1:T(8,128)}, u32[]{:S(2)}) copy-start(f32[256,2,2,64]{0,3,2,1:T(8,128)} %copy.175) | copy-start | bytes 786436
  184.2 9.7 %copy-start.31 = (f32[256,2,2,64]{0,3,2,1:T(8,128)S(1)}, f32[256,2,2,64]{0,3,2,1:T(8,128)}, u32[]{:S(2)}) copy-start(f32[256,2,2,64]{0,3,2,1:T(8,128)} %copy.171) | copy-start | bytes 786436
  184.2 9.7 %copy-start.32 = (f32[256,2,2,64]{0,3,2,1:T(8,128)S(1)}, f32[256,2,2,64]{0,3,2,1:T(8,128)}, u32[]{:S(2)}) copy-start(f32[256,2,2,64]{0,3,2,1:T(8,128)} %copy.169) | copy-start | bytes 786436
  184.3 9.7 %copy-start.33 = (f32[256,2,2,64]{0,3,2,1:T(8,128)S(1)}, f32[256,2,2,64]{0,3,2,1:T(8,128)}, u32[]{:S(2)}) copy-start(f32[256,2,2,64]{0,3,2,1:T(8,128)} %copy.164) | copy-start | bytes 786436
  184.3 9.7 %copy-start.34 = (f32[256,2,2,64]{0,3,2,1:T(8,128)S(1)}, f32[256,2,2,64]{0,3,2,1:T(8,128)}, u32[]{:S(2)}) copy-start(f32[256,2,2,64]{0,3,2,1:T(8,128)} %copy.162) | copy-start | bytes 786436
  184.3 9.7 %copy-start.35 = (f32[256,2,2,64]{0,3,2,1:T(8,128)S(1)}, f32[256,2,2,64]{0,3,2,1:T(8,128)}, u32[]{:S(2)}) copy-start(f32[256,2,2,64]{0,3,2,1:T(8,128)} %copy.154) | copy-start | bytes 786436
  184.3 9.7 %copy-start.36 = (f32[256,2,2,64]{0,3,2,1:T(8,128)S(1)}, f32[256,2,2,64]{0,3,2,1:T(8,128)}, u32[]{:S(2)}) copy-start(f32[256,2,2,64]{0,3,2,1:T(8,128)} %copy.156) | copy-start | bytes 786436
  184.3 9.7 %copy-start.37 = (f32[256,2,2,64]{0,3,2,1:T(8,128)S(1)}, f32[256,2,2,64]{0,3,2,1:T(8,128)}, u32[]{:S(2)}) copy-start(f32[256,2,2,64]{0,3,2,1:T(8,128)} %copy.152) | copy-start | bytes 786436
  216.4 109.2 %all-reduce.2.cloned.1.call-start = ((), (), s32[]{:S(2)}) async-start(), calls=%async_computation.3 | async-start | bytes 1048576 | tf_op jit(solution)/shard_map/psum | solution.py:197
  (28 other events, 84.2 us)
Sparse Core Ops, SparseCore 0:
  216.5 32.8 reduce-scatter.1
  252.8 72.7 all-reduce.1
where the time goes:
time: 337 us; the launch traced here: 334 us
  local copies, waits for them, and re-layouts  121 us (36%)
  waiting for transfers between devices  119 us (35%)
  other arithmetic  56 us (17%)
  between operations  18.3 us (5%)
  starting transfers between devices  14.8 us (4%)
  matrix products  4.74 us (1%)
    psum x1, waiting for transfers between devices, body(): summed = lax.psum(partial_sums, ('gz', 'gy'))  76.2 us
    mul x25, local copies, waits for them, and re-layouts, apply_link(): out_real = out_real + coeff_real * value_real - coeff_imag * value_imag  38.5 us
    reduce_scatter x1, waiting for transfers between devices, body(): lax.psum_scatter(contract(transformed_rows, stacked_left), 'vec', scatter...  33 us
    mul x21, local copies, waits for them, and re-layouts, apply_adjoint(): out_real = out_real + coeff_real * value_real + coeff_imag * value_imag  28.9 us
    another operation x4, other arithmetic  17.4 us
    convert_element_type x1, other arithmetic, stencil_lists(): padded.astype(jnp.float32)  12.6 us
    concatenate x5, local copies, waits for them, and re-layouts, extended(): block = jnp.concatenate([low, block, high], axis=dim)  12.5 us
    slice x1, local copies, waits for them, and re-layouts, stencil_lists(): pad_imag = widened[..., 1, :]  10.1 us
  transfers between devices with their start and end apart: 9, of which 4 were waited for; matrix products, arithmetic and copies ran while one was open for 12% of the time, Pallas kernels for 0%

commit v1 on v0

v1 whole, which is shorter than its diff:
```python
import functools
import math

import jax
import jax.numpy as jnp
from jax import lax
from jax.experimental import pallas as pl
from jax.experimental.pallas import tpu as pltpu
from jax.sharding import PartitionSpec as P

MESH = pl.DeviceIdType.MESH


def split_chunks(depth, most):
    count = most
    while depth % count:
        count -= 1
    return count


def kernel(
    sizes,
    v_ref,
    tabx_ref,
    taby_ref,
    tabz_ref,
    phase_ref,
    out_ref,
    ext,
    left,
    ty,
    tz,
    trans,
    acc,
    outgo,
    income,
    reduced,
    local_sem,
    send_sem,
    recv_sem,
    red_sem,
):
    gz_n, gy_n, vec_n, depth, height, rows, width, chunks = sizes
    pairs = vec_n // 2
    lanes = 2 * width
    me_z = lax.axis_index("gz")
    me_y = lax.axis_index("gy")
    me_v = lax.axis_index("vec")
    pair = me_v // 2
    side = lax.rem(me_v, 2)
    group = gz_n * gy_n
    me_g = me_z * gy_n + me_y

    def member(step):
        return lax.rem(me_g + step, group)

    def place(g):
        return {"gz": g // gy_n, "gy": lax.rem(g, gy_n)}

    centre = ext.at[pl.ds(1, depth), pl.ds(1, height)]
    locals_ = [
        pltpu.make_async_copy(v_ref, centre, local_sem.at[0]),
        pltpu.make_async_copy(v_ref, left.at[pair, side], local_sem.at[1]),
        pltpu.make_async_copy(taby_ref, ty.at[:, pl.ds(1, height)], local_sem.at[2]),
        pltpu.make_async_copy(tabz_ref, tz.at[pl.ds(1, depth)], local_sem.at[3]),
    ]
    for copy in locals_:
        copy.start()

    barrier = pltpu.get_barrier_semaphore()
    for step in range(1, group):
        pl.semaphore_signal(barrier, inc=1, device_id=place(member(step)), device_id_type=MESH)
    for step in range(1, vec_n):
        pl.semaphore_signal(
            barrier, inc=1, device_id={"vec": lax.rem(me_v + step, vec_n)}, device_id_type=MESH
        )
    pl.semaphore_wait(barrier, group - 1 + vec_n - 1)

    counter = [0]

    def remote(src, dst, device):
        index = counter[0]
        counter[0] += 1
        return pltpu.make_async_remote_copy(
            src_ref=src,
            dst_ref=dst,
            send_sem=send_sem.at[index],
            recv_sem=recv_sem.at[index],
            device_id=device,
            device_id_type=MESH,
        )

    z_up = {"gz": lax.rem(me_z + 1, gz_n)}
    z_down = {"gz": lax.rem(me_z + gz_n - 1, gz_n)}
    y_up = {"gy": lax.rem(me_y + 1, gy_n)}
    y_down = {"gy": lax.rem(me_y + gy_n - 1, gy_n)}
    sibling = {"vec": pair * 2 + 1 - side}
    inner_z = pl.ds(1, depth)
    inner_y = pl.ds(1, height)
    z_copies = [
        remote(v_ref.at[depth - 1], ext.at[0, inner_y], z_up),
        remote(v_ref.at[0], ext.at[depth + 1, inner_y], z_down),
        remote(tabz_ref.at[depth - 1], tz.at[0], z_up),
    ]
    y_copies = [
        remote(v_ref.at[:, height - 1], ext.at[inner_z, 0], y_up),
        remote(v_ref.at[:, 0], ext.at[inner_z, height + 1], y_down),
        remote(taby_ref.at[:, height - 1], ty.at[:, 0], y_up),
    ]
    near = remote(v_ref, left.at[pair, side], sibling)
    span = depth // chunks
    far = []
    relay = []
    for k in range(chunks):
        part = pl.ds(k * span, span)
        for hop in range(1, pairs):
            target = lax.rem(pair + hop, pairs)
            source = lax.rem(pair + pairs - hop, pairs)
            far.append(
                remote(
                    v_ref.at[part], left.at[pair, side, part], {"vec": target * 2 + side}
                )
            )
            relay.append(
                remote(left.at[source, side, part], left.at[source, side, part], sibling)
            )
    for copy in z_copies:
        copy.start()
    for copy in far[: pairs - 1]:
        copy.start()
    for copy in y_copies:
        copy.start()
    for copy in far[pairs - 1 :]:
        copy.start()
    near.start()

    lane = lax.broadcasted_iota(jnp.int32, (1, lanes), 1)
    last_mask = lax.rem(lane, width) == width - 1
    first_mask = lax.rem(lane, width) == 0
    sign = jnp.where(lane < width, 1.0, -1.0).astype(jnp.float32)
    tile = 32 if rows % 32 == 0 else rows

    def store(z, y, colour, slot, lo, value):
        turned = pltpu.roll(value, width, 1) * sign
        trans[z, y, colour, pl.ds(slot * 2 * rows + lo, tile)] = value.astype(jnp.bfloat16)
        trans[z, y, colour, pl.ds((slot * 2 + 1) * rows + lo, tile)] = turned.astype(jnp.bfloat16)

    def load(z, y, colour, lo):
        return ext[z, y, colour, pl.ds(lo, tile)].astype(jnp.float32)

    def stencil(z, y, lo, slot, ahead, behind, up, down):
        sums = [0.0, 0.0, 0.0]
        for col in range(3):
            value, swapped = ahead(col)
            for row in range(3):
                k = row * 3 + col
                sums[row] = sums[row] + (up(k) * value + up(9 + k) * swapped)
        for col in range(3):
            value, swapped = behind(col)
            for row in range(3):
                k = col * 3 + row
                sums[row] = sums[row] + (down(9 + k) * swapped - down(k) * value)
        for row in range(3):
            store(z, y, row, slot, lo, sums[row])

    def swap(value):
        return value, pltpu.roll(value, width, 1)

    def pass_x(z):
        for y in range(height):
            for lo in range(0, rows, tile):
                cosine = phase_ref[z, y, 0:1]
                sine = phase_ref[z, y, 1:2]

                def ahead(col):
                    value = load(z + 1, y + 1, col, lo)
                    one = pltpu.roll(value, lanes - 1, 1)
                    two = pltpu.roll(value, width - 1, 1)
                    return jnp.where(last_mask, two, one), jnp.where(last_mask, one, two)

                def behind(col):
                    value = load(z + 1, y + 1, col, lo)
                    one = pltpu.roll(value, 1, 1)
                    two = pltpu.roll(value, width + 1, 1)
                    return jnp.where(first_mask, two, one), jnp.where(first_mask, one, two)

                stencil(
                    z, y, lo, 0, ahead, behind,
                    lambda k: tabx_ref[0, z, y, k : k + 1],
                    lambda k: tabx_ref[1, z, y, k : k + 1],
                )
                for col in range(3):
                    value, swapped = swap(load(z + 1, y + 1, col, lo))
                    store(z, y, col, 3, lo, value * cosine + swapped * sine)

    def pass_y(z):
        for y in range(height):
            for lo in range(0, rows, tile):
                stencil(
                    z, y, lo, 1,
                    lambda col: swap(load(z + 1, y + 2, col, lo)),
                    lambda col: swap(load(z + 1, y, col, lo)),
                    lambda k: ty[z, y + 1, k : k + 1],
                    lambda k: ty[z, y, k : k + 1],
                )

    def pass_z(z):
        for y in range(height):
            for lo in range(0, rows, tile):
                stencil(
                    z, y, lo, 2,
                    lambda col: swap(load(z + 2, y + 1, col, lo)),
                    lambda col: swap(load(z, y + 1, col, lo)),
                    lambda k: tz[z + 1, y, k : k + 1],
                    lambda k: tz[z, y, k : k + 1],
                )

    for copy in locals_:
        copy.wait()
    pl.loop(0, depth)(pass_x)
    for copy in z_copies:
        copy.wait()
    pl.loop(0, depth)(pass_z)
    for copy in y_copies:
        copy.wait()
    pl.loop(0, depth)(pass_y)

    share = 8 * rows // group

    def contract(which, z, fresh):
        sites = [(y, c) for y in range(height) for c in range(3)]
        a = jnp.concatenate([trans[z, y, c] for y, c in sites], axis=1)
        b = jnp.concatenate(
            [
                jnp.concatenate([left[which, s, z, y, c] for y, c in sites], axis=1)
                for s in range(2)
            ],
            axis=0,
        )
        product = lax.dot_general(
            a, b, (((1,), (1,)), ((), ())), preferred_element_type=jnp.float32
        ).reshape(group, share, 2 * rows)
        columns = pl.ds(pl.multiple_of(which * 2 * rows, 2 * rows), 2 * rows)
        if fresh:
            acc[:, :, columns] = product
        else:
            acc[:, :, columns] += product

    def contract_range(which, lo, hi):
        start = lo
        if lo == 0:
            contract(which, 0, True)
            start = 1
        if hi > start:
            pl.loop(start, hi)(lambda z: contract(which, z, False))

    near.wait()
    contract_range(pair, 0, depth)
    for k in range(chunks):
        for hop in range(1, pairs):
            index = k * (pairs - 1) + hop - 1
            far[index].wait()
            relay[index].start()
        if k:
            for hop in range(1, pairs):
                relay[(k - 1) * (pairs - 1) + hop - 1].wait()
                contract_range(
                    lax.rem(pair + pairs - hop, pairs), (k - 1) * span, k * span
                )
    for hop in range(1, pairs):
        relay[(chunks - 1) * (pairs - 1) + hop - 1].wait()
        contract_range(lax.rem(pair + pairs - hop, pairs), (chunks - 1) * span, depth)

    outgo[...] = acc[...].astype(jnp.bfloat16)
    scatter = []
    for step in range(1, group):
        g = member(step)
        copy = pltpu.make_async_remote_copy(
            src_ref=outgo.at[g],
            dst_ref=income.at[me_g],
            send_sem=red_sem.at[0, step],
            recv_sem=red_sem.at[1, step],
            device_id=place(g),
            device_id_type=MESH,
        )
        copy.start()
        scatter.append(copy)
    for copy in scatter:
        copy.wait()
    total = acc[me_g]
    for step in range(1, group):
        total = total + income[member(step)].astype(jnp.float32)
    reduced[...] = total.astype(jnp.bfloat16)
    out_ref[me_g] = total.astype(jnp.bfloat16)
    gather = []
    for step in range(1, group):
        g = member(step)
        copy = pltpu.make_async_remote_copy(
            src_ref=reduced,
            dst_ref=out_ref.at[me_g],
            send_sem=red_sem.at[2, step],
            recv_sem=red_sem.at[3, step],
            device_id=place(g),
            device_id_type=MESH,
        )
        copy.start()
        gather.append(copy)
    for copy in gather:
        copy.wait()


def link_table(real, imag):
    first = jnp.concatenate([real, real], -1)
    second = jnp.concatenate([-imag, imag], -1)
    both = jnp.stack([first, second], 0) * 0.5
    both = jnp.transpose(both, (3, 4, 0, 1, 2, 5))
    depth, height = both.shape[:2]
    return both.reshape(depth, height, 18, both.shape[-1])


def body(vectors, links, momentum, directions):
    rows, _, depth, height, lanes = vectors.shape
    width = lanes // 2
    gz_n = lax.axis_size("gz")
    gy_n = lax.axis_size("gy")
    vec_n = lax.axis_size("vec")
    group = gz_n * gy_n
    extent_y = height * gy_n
    extent_z = depth * gz_n
    chunks = split_chunks(depth, 4)

    v = jnp.transpose(vectors, (2, 3, 1, 0, 4))
    wide = links.astype(jnp.float32).reshape(3, 3, 3, depth, height, 2, width)
    real = wide[..., 0, :]
    imag = wide[..., 1, :]
    tabx = jnp.stack(
        [
            link_table(real[0], imag[0]),
            link_table(jnp.roll(real[0], 1, -1), jnp.roll(imag[0], 1, -1)),
        ]
    )
    taby = link_table(real[1], imag[1])
    tabz = link_table(real[2], imag[2])

    x = jnp.arange(width, dtype=jnp.int32)
    y = lax.axis_index("gy") * height + jnp.arange(height, dtype=jnp.int32)
    z = lax.axis_index("gz") * depth + jnp.arange(depth, dtype=jnp.int32)
    frac_x = (momentum[0] * x % width).astype(jnp.float32) / width
    frac_y = (momentum[1] * y % extent_y).astype(jnp.float32) / extent_y
    frac_z = (momentum[2] * z % extent_z).astype(jnp.float32) / extent_z
    summed = frac_z[:, None, None] + frac_y[None, :, None] + frac_x[None, None, :]
    angle = 2.0 * math.pi * summed
    cosine, sine = jnp.cos(angle), jnp.sin(angle)
    phase = jnp.stack(
        [jnp.concatenate([cosine, cosine], -1), jnp.concatenate([sine, -sine], -1)], 2
    )

    share = 8 * rows // group
    bf16, f32 = jnp.bfloat16, jnp.float32
    remote_count = 7 + 2 * chunks * (vec_n // 2 - 1)
    vmem = pl.BlockSpec(memory_space=pltpu.VMEM)
    hbm = pl.BlockSpec(memory_space=pl.ANY)
    sizes = (gz_n, gy_n, vec_n, depth, height, rows, width, chunks)
    out = pl.pallas_call(
        functools.partial(kernel, sizes),
        out_shape=jax.ShapeDtypeStruct((group, share, vec_n * rows), bf16),
        in_specs=[hbm, vmem, hbm, hbm, vmem],
        out_specs=vmem,
        scratch_shapes=[
            pltpu.VMEM((depth + 2, height + 2, 3, rows, lanes), bf16),
            pltpu.VMEM((vec_n // 2, 2, depth, height, 3, rows, lanes), bf16),
            pltpu.VMEM((depth, height + 1, 18, lanes), f32),
            pltpu.VMEM((depth + 1, height, 18, lanes), f32),
            pltpu.VMEM((depth, height, 3, 8 * rows, lanes), bf16),
            pltpu.VMEM((group, share, vec_n * rows), f32),
            pltpu.VMEM((group, share, vec_n * rows), bf16),
            pltpu.VMEM((group, share, vec_n * rows), bf16),
            pltpu.VMEM((share, vec_n * rows), bf16),
            pltpu.SemaphoreType.DMA((4,)),
            pltpu.SemaphoreType.DMA((remote_count,)),
            pltpu.SemaphoreType.DMA((remote_count,)),
            pltpu.SemaphoreType.DMA((4, group)),
        ],
        compiler_params=pltpu.CompilerParams(
            collective_id=0, has_side_effects=True, vmem_limit_bytes=48 * 1024 * 1024
        ),
    )(v, tabx, taby, tabz, phase)

    scale = 1.0 / math.sqrt(width * extent_y * extent_z)
    derived = out.reshape(4, 2, rows, vec_n * rows)
    parts = []
    for slot in range(3):
        chosen = directions[slot]
        parts.append(
            jnp.where(chosen == 0, derived[0], jnp.where(chosen == 1, derived[1], derived[2]))
        )
    parts.append(derived[3])
    return jnp.stack(parts).astype(f32) * scale


def solution(mesh):
    in_specs = (P("vec", None, "gz", "gy", None), P(None, None, None, "gz", "gy", None), P(), P())
    out_specs = P(None, None, "vec", None)
    return jax.shard_map(body, mesh=mesh, in_specs=in_specs, out_specs=out_specs, check_vma=False)
```

time: 337 us -> 62.9 us (0.19)
  waiting for transfers between devices: 119 us -> 0 us
  local copies, waits for them, and re-layouts: 121 us -> 4.73 us
  other arithmetic: 56 us -> 3.88 us
  Pallas kernels: 0 us -> 49.9 us
  starting transfers between devices: 14.8 us -> 0 us
  between operations: 18.3 us -> 4.08 us
  matrix products: 4.74 us -> 0 us
    psum x1 -> x0, waiting for transfers between devices: 76.2 us -> none  [body(): summed = lax.psum(partial_sums, ('gz', 'gy'))]
    mul x46 -> x0, local copies, waits for them, and re-layouts: 67.4 us -> none  [the longest x25 38.5 us: apply_link(): out_real = out_real + coeff_real * value_real - coeff_imag * value_imag]
    pallas_call x0 -> x1, Pallas kernels: none -> 49.9 us  [body(): pl.pallas_call(functools.partial(kernel, sizes), out_shape=jax.ShapeDtype...]
    reduce_scatter x1 -> x0, waiting for transfers between devices: 33 us -> none  [body(): lax.psum_scatter(contract(transformed_rows, stacked_left), 'vec', scatter...]
    another operation x10 -> x8, other arithmetic: 25.8 us -> 0.61 us  [the longest x5 0.53 us: link_table(): both = jnp.stack([first, second], 0) * 0.5]
    slice x14 -> x5, local copies, waits for them, and re-layouts: 18.3 us -> 1.66 us  [the longest x1 0.61 us: body(): chosen = directions[slot]]
    convert_element_type x6 -> x0, other arithmetic: 12.8 us -> none  [the longest x1 12.6 us: stencil_lists(): padded.astype(jnp.float32)]
    concatenate x5 -> x0, local copies, waits for them, and re-layouts: 12.5 us -> none  [extended(): block = jnp.concatenate([low, block, high], axis=dim)]
  transfers between devices with their start and end apart: 9 -> 0, of which waited for: 4 -> 0; matrix products, arithmetic and copies ran while one was open for 12% -> 0% of each run, Pallas kernels for 0% -> 0%
where the time goes in v1:
time: 62.9 us; the launch traced here: 62.6 us
  Pallas kernels  49.9 us (79%)
  local copies, waits for them, and re-layouts  4.73 us (8%)
  between operations  4.08 us (6%)
  other arithmetic  3.88 us (6%)
    pallas_call x1, Pallas kernels, body(): pl.pallas_call(functools.partial(kernel, sizes), out_shape=jax.ShapeDtype...  49.9 us
    unnamed x7, local copies, waits for them, and re-layouts  1.69 us

profile of v1, /device:TPU:0, one launch (start us, length us, event | category | flops | bytes accessed | tf_op | source)
XLA Modules:
  0.0 62.6 jit_solution(3070162112641422570)
XLA Ops:
  0.0 0.9 %copy.29 = f32[3,3,3,8,2,128]{5,3,4,2,1,0:T(8,128)S(1)} copy(bf16[3,3,3,8,2,128]{5,4,3,2,1,0:T(2,128)(2,1)} %param.5) | data formatting | bytes 331776 | tf_op jit(solution)/shard_map/reshape | solution.py:333
  0.9 0.3 reshape.134
  1.2 0.3 fusion.12
  1.5 0.1 slice.116
  1.6 0.1 maximum_negate_fusion
  1.7 0.1 maximum_bitcast_fusion.3
  1.8 0.1 slice.114
  1.9 0.1 maximum_bitcast_fusion
  2.0 0.1 maximum_bitcast_fusion.1
  2.2 0.1 copy.34
  2.2 0.1 copy.35
  2.3 0.0 copy-start.1
  2.3 0.6 copy-done.1
  2.9 0.6 fusion.14
  3.5 0.7 %fusion.3 = f32[8]{0:T(128)S(1)} fusion(s32[]{:T(128)S(6)} %mul.65, s32[]{:T(128)} %bitcast.24), kind=kLoop, calls=%fused_computation.37 | loop fusion | flops 120 | bytes 40 | tf_op jit(solution)/shard_map/div | solution.py:350
  4.2 0.6 fusion.5
  4.8 0.1 broadcast_add_fusion
  4.8 0.6 %fusion.7 = f32[64]{0:T(128)S(1)} fusion(s32[]{:T(128)} %bitcast.26), kind=kLoop, calls=%fused_computation.41 | loop fusion | flops 896 | bytes 260 | tf_op jit(solution)/shard_map/div | solution.py:348
  5.5 0.2 fusion.1
  5.7 0.1 pad_maximum_fusion.2
  5.8 0.1 maximum_bitcast_fusion.6
  6.0 0.0 copy-start
  6.0 0.1 copy.43.tabz_ref
  6.1 0.1 maximum_bitcast_fusion.4
  6.2 0.1 copy.42.taby_ref
  6.2 0.9 %copy-done = bf16[64,3,8,2,128]{4,3,2,1,0:T(2,128)(2,1)S(1)} copy-done((bf16[64,3,8,2,128]{4,3,2,1,0:T(2,128)(2,1)S(1)}, bf16[64,3,8,2,128]{4,3,2,1,0:T(2,128)(2,1)}, u32[]{:S(2)}) %copy-start) | copy-done | bytes 786456
  7.1 0.2 copy.58
  7.3 0.0 copy-start.2
  7.3 49.9 %shard_map.46 = bf16[8,64,256]{2,1,0:T(8,128)(2,1)S(1)} custom-call(bf16[8,2,3,64,128]{4,3,2,1,0:T(8,128)(2,1)S(1)} %bitcast.74, f32[2,8,2,18,128]{4,3,2,1,0:T(8,128)S(1)} %pad_maximum_fusion.tabx_ref, f32[8,2,18,128]{3,2,1,0:T(8,128)S(1)} %copy.42.taby_ref, f32[8,2,18,128]{3,2,1,0:T(8,128)S(1)} %copy.43.tabz_ref, ...), custom_call_target="tpu_custom_call" | custom-call | tf_op jit(solution)/shard_map/pallas_call | solution.py:364
  57.3 0.0 copy-done.2
  57.3 0.6 fusion.13
  61.8 0.9 %convert_multiply_fusion = f32[4,2,64,256]{3,2,1,0:T(8,128)} fusion(bf16[1,2,64,256]{3,2,1,0:T(8,128)(2,1)S(1)} %get-tuple-element.12, bf16[1,2,64,256]{3,2,1,0:T(8,128)(2,1)S(1)} %get-tuple-element.14, bf16[1,2,64,256]{3,2,1,0:T(8,128)(2,1)S(1)} %get-tuple-element.13, bf16[1,2,64,256]{3,2,1,0:T(8,128)(2,1)S(1)} %get-tuple-element.11), kind=kLoop, calls=%fused_computation.1 | loop fusion | flops 655360 | bytes 786432 | tf_op jit(solution)/shard_map/mul | solution.py:398
  (9 shorter events, 0.2 us)
Async XLA Ops:
  2.3 0.7 %copy-start.1 = (s32[3]{0:T(128)S(1)}, s32[3]{0:T(128)}, u32[]{:S(2)}) copy-start(s32[3]{0:T(128)} %param.6) | copy-start | bytes 40
  6.0 1.1 %copy-start = (bf16[64,3,8,2,128]{4,3,2,1,0:T(2,128)(2,1)S(1)}, bf16[64,3,8,2,128]{4,3,2,1,0:T(2,128)(2,1)}, u32[]{:S(2)}) copy-start(bf16[64,3,8,2,128]{4,3,2,1,0:T(2,128)(2,1)} %param.4) | copy-start | bytes 2359300
  7.3 50.0 %copy-start.2 = (s32[3]{0:T(128)S(1)}, s32[3]{0:T(128)}, u32[]{:S(2)}) copy-start(s32[3]{0:T(128)} %param.7) | copy-start | bytes 40

commit v2 on v1

v2 whole, which is shorter than its diff:
```python
import functools
import math

import jax
import jax.numpy as jnp
from jax import lax
from jax.experimental import pallas as pl
from jax.experimental.pallas import tpu as pltpu
from jax.sharding import PartitionSpec as P

MESH = pl.DeviceIdType.MESH


def split_chunks(depth, most):
    count = most
    while depth % count:
        count -= 1
    return count


def kernel(
    sizes,
    momentum_ref,
    directions_ref,
    v_ref,
    links_ref,
    links_far,
    out_ref,
    ext,
    left,
    rim_y,
    rim_z,
    tab_x,
    tab_y,
    tab_z,
    cos_ref,
    sin_ref,
    trans,
    acc,
    outgo,
    income,
    reduced,
    gathered,
    local_sem,
    send_sem,
    recv_sem,
    red_sem,
):
    gz_n, gy_n, vec_n, depth, height, rows, width, chunks = sizes
    pairs = vec_n // 2
    lanes = 2 * width
    me_z = lax.axis_index("gz")
    me_y = lax.axis_index("gy")
    me_v = lax.axis_index("vec")
    pair = me_v // 2
    side = lax.rem(me_v, 2)
    group = gz_n * gy_n
    me_g = me_z * gy_n + me_y
    span = depth // chunks

    def member(step):
        return lax.rem(me_g + step, group)

    def place(g):
        return {"gz": g // gy_n, "gy": lax.rem(g, gy_n)}

    barrier = pltpu.get_barrier_semaphore()
    for step in range(1, group):
        pl.semaphore_signal(barrier, inc=1, device_id=place(member(step)), device_id_type=MESH)
    for step in range(1, vec_n):
        pl.semaphore_signal(
            barrier, inc=1, device_id={"vec": lax.rem(me_v + step, vec_n)}, device_id_type=MESH
        )
    centre = ext.at[pl.ds(1, depth), pl.ds(1, height)]
    locals_ = [
        pltpu.make_async_copy(v_ref, centre, local_sem.at[0]),
        pltpu.make_async_copy(v_ref, left.at[pair, side], local_sem.at[1]),
    ]
    for copy in locals_:
        copy.start()
    pl.semaphore_wait(barrier, group - 1 + vec_n - 1)

    counter = [0]

    def remote(src, dst, device):
        index = counter[0]
        counter[0] += 1
        return pltpu.make_async_remote_copy(
            src_ref=src,
            dst_ref=dst,
            send_sem=send_sem.at[index],
            recv_sem=recv_sem.at[index],
            device_id=device,
            device_id_type=MESH,
        )

    z_up = {"gz": lax.rem(me_z + 1, gz_n)}
    z_down = {"gz": lax.rem(me_z + gz_n - 1, gz_n)}
    y_up = {"gy": lax.rem(me_y + 1, gy_n)}
    y_down = {"gy": lax.rem(me_y + gy_n - 1, gy_n)}
    sibling = {"vec": pair * 2 + 1 - side}
    inner_y = pl.ds(1, height)
    z_copies = [
        remote(v_ref.at[depth - 1], ext.at[0, inner_y], z_up),
        remote(v_ref.at[0], ext.at[depth + 1, inner_y], z_down),
        remote(links_far.at[2, depth - 1], rim_z, z_up),
    ]
    rim_copy = remote(links_far.at[1, :, height - 1], rim_y, y_up)
    near = remote(v_ref, left.at[pair, side], sibling)
    far, relay, y_copies = [], [], []
    for k in range(chunks):
        part = pl.ds(k * span, span)
        inner_z = pl.ds(1 + k * span, span)
        y_copies.append(
            (
                remote(v_ref.at[part, height - 1], ext.at[inner_z, 0], y_up),
                remote(v_ref.at[part, 0], ext.at[inner_z, height + 1], y_down),
            )
        )
        for hop in range(1, pairs):
            target = lax.rem(pair + hop, pairs)
            source = lax.rem(pair + pairs - hop, pairs)
            far.append(
                remote(v_ref.at[part], left.at[pair, side, part], {"vec": target * 2 + side})
            )
            relay.append(
                remote(left.at[source, side, part], left.at[source, side, part], sibling)
            )
    rim_copy.start()
    for copy in z_copies:
        copy.start()
    for k in range(chunks):
        for copy in far[k * (pairs - 1) : (k + 1) * (pairs - 1)]:
            copy.start()
        for copy in y_copies[k]:
            copy.start()
    near.start()

    lane = lax.broadcasted_iota(jnp.int32, (1, lanes), 1)
    low_half = lane < width
    last_mask = lax.rem(lane, width) == width - 1
    first_mask = lax.rem(lane, width) == 0
    sign = jnp.where(low_half, 1.0, -1.0).astype(jnp.float32)
    tile = 32 if rows % 32 == 0 else rows

    site_shape = (depth * height, lanes)
    site = lax.broadcasted_iota(jnp.int32, site_shape, 0)
    x_at = lax.rem(lax.broadcasted_iota(jnp.int32, site_shape, 1), width)
    y_at = me_y * height + lax.rem(site, height)
    z_at = me_z * depth + site // height

    def fraction(component, at, extent):
        turned = lax.rem(momentum_ref[component] * at, extent)
        turned = jnp.where(turned < 0, turned + extent, turned)
        return turned.astype(jnp.float32) / extent

    angle = (2.0 * math.pi) * (
        fraction(2, z_at, depth * gz_n)
        + fraction(1, y_at, height * gy_n)
        + fraction(0, x_at, width)
    )
    cos_ref[...] = jnp.cos(angle)
    sin_ref[...] = jnp.sin(angle) * sign

    def coefficients(raw):
        value = raw.astype(jnp.float32) * 0.5
        swapped = pltpu.roll(value, width, 1)
        real = jnp.where(low_half, value, swapped)
        imag = jnp.where(low_half, -swapped, value)
        return real, imag

    def put(table, where, pair_of):
        table[where + (slice(0, 9),)] = pair_of[0]
        table[where + (slice(16, 25),)] = pair_of[1]

    def step_back(value):
        one = pltpu.roll(value, 1, 1)
        two = pltpu.roll(value, width + 1, 1)
        return jnp.where(first_mask, two, one)

    def make_tables(z):
        for y in range(height):
            real, imag = coefficients(links_ref[0, z, y])
            put(tab_x, (0, z, y), (real, imag))
            put(tab_x, (1, z, y), (step_back(real), step_back(imag)))
            put(tab_y, (z, y + 1), coefficients(links_ref[1, z, y]))
            put(tab_z, (z + 1, y), coefficients(links_ref[2, z, y]))

    pl.loop(0, depth)(make_tables)

    def store(z, y, colour, slot, lo, value):
        turned = pltpu.roll(value, width, 1) * sign
        trans[z, y, colour, pl.ds(slot * 2 * rows + lo, tile)] = value.astype(jnp.bfloat16)
        trans[z, y, colour, pl.ds((slot * 2 + 1) * rows + lo, tile)] = turned.astype(jnp.bfloat16)

    def load(z, y, colour, lo):
        return ext[z, y, colour, pl.ds(lo, tile)].astype(jnp.float32)

    def stencil(z, y, lo, slot, ahead, behind, up, down):
        sums = [0.0, 0.0, 0.0]
        for col in range(3):
            value, swapped = ahead(col)
            for row in range(3):
                k = row * 3 + col
                sums[row] = sums[row] + (up(k) * value + up(16 + k) * swapped)
        for col in range(3):
            value, swapped = behind(col)
            for row in range(3):
                k = col * 3 + row
                sums[row] = sums[row] + (down(16 + k) * swapped - down(k) * value)
        for row in range(3):
            store(z, y, row, slot, lo, sums[row])

    def swap(value):
        return value, pltpu.roll(value, width, 1)

    def pass_x(z):
        for y in range(height):
            for lo in range(0, rows, tile):
                here = pl.ds(z * height + y, 1)
                cosine = cos_ref[here]
                sine = sin_ref[here]

                def ahead(col):
                    value = load(z + 1, y + 1, col, lo)
                    one = pltpu.roll(value, lanes - 1, 1)
                    two = pltpu.roll(value, width - 1, 1)
                    return jnp.where(last_mask, two, one), jnp.where(last_mask, one, two)

                def behind(col):
                    value = load(z + 1, y + 1, col, lo)
                    one = pltpu.roll(value, 1, 1)
                    two = pltpu.roll(value, width + 1, 1)
                    return jnp.where(first_mask, two, one), jnp.where(first_mask, one, two)

                stencil(
                    z, y, lo, 0, ahead, behind,
                    lambda k: tab_x[0, z, y, k : k + 1],
                    lambda k: tab_x[1, z, y, k : k + 1],
                )
                for col in range(3):
                    value, swapped = swap(load(z + 1, y + 1, col, lo))
                    store(z, y, col, 2, lo, value * cosine + swapped * sine)

    def pass_y(z):
        for y in range(height):
            for lo in range(0, rows, tile):
                stencil(
                    z, y, lo, 3,
                    lambda col: swap(load(z + 1, y + 2, col, lo)),
                    lambda col: swap(load(z + 1, y, col, lo)),
                    lambda k: tab_y[z, y + 1, k : k + 1],
                    lambda k: tab_y[z, y, k : k + 1],
                )

    def pass_z(z):
        for y in range(height):
            for lo in range(0, rows, tile):
                stencil(
                    z, y, lo, 1,
                    lambda col: swap(load(z + 2, y + 1, col, lo)),
                    lambda col: swap(load(z, y + 1, col, lo)),
                    lambda k: tab_z[z + 1, y, k : k + 1],
                    lambda k: tab_z[z, y, k : k + 1],
                )

    def contract(which, chunk, lo, hi, fresh):
        sites = [
            (chunk * span + dz, y, c) for dz in range(span) for y in range(height) for c in range(3)
        ]
        a = jnp.concatenate([trans[z, y, c, lo:hi] for z, y, c in sites], axis=1)
        b = jnp.concatenate(
            [
                jnp.concatenate([left[which, s, z, y, c] for z, y, c in sites], axis=1)
                for s in range(2)
            ],
            axis=0,
        )
        product = lax.dot_general(
            a, b, (((1,), (1,)), ((), ())), preferred_element_type=jnp.float32
        )
        columns = pl.ds(pl.multiple_of(which * 2 * rows, 2 * rows), 2 * rows)
        if fresh:
            acc[lo:hi, columns] = product
        else:
            acc[lo:hi, columns] += product

    for copy in locals_:
        copy.wait()
    pl.loop(0, depth)(pass_x)
    for copy in z_copies:
        copy.wait()
    for y in range(height):
        put(tab_z, (0, y), coefficients(rim_z[y]))
    pl.loop(0, depth)(pass_z)

    early = 6 * rows
    near.wait()
    contract(pair, 0, 0, early, True)
    pl.loop(1, chunks)(lambda k: contract(pair, k, 0, early, False))

    rim_copy.wait()

    @pl.loop(0, depth)
    def _(z):
        put(tab_y, (z, 0), coefficients(rim_y[z]))

    for k in range(chunks + 1):
        if k < chunks:
            for copy in y_copies[k]:
                copy.wait()
            pl.loop(k * span, (k + 1) * span)(pass_y)
            contract(pair, k, early, 8 * rows, k == 0)
            for hop in range(1, pairs):
                index = k * (pairs - 1) + hop - 1
                far[index].wait()
                relay[index].start()
        if k:
            for hop in range(1, pairs):
                relay[(k - 1) * (pairs - 1) + hop - 1].wait()
                contract(lax.rem(pair + pairs - hop, pairs), k - 1, 0, 8 * rows, k == 1)

    share = 8 * rows // group
    outgo[...] = acc[...].reshape(outgo.shape).astype(jnp.bfloat16)
    scatter = []
    for step in range(1, group):
        g = member(step)
        copy = pltpu.make_async_remote_copy(
            src_ref=outgo.at[g],
            dst_ref=income.at[me_g],
            send_sem=red_sem.at[0, step],
            recv_sem=red_sem.at[1, step],
            device_id=place(g),
            device_id_type=MESH,
        )
        copy.start()
        scatter.append(copy)
    for copy in scatter:
        copy.wait()
    total = acc[pl.ds(pl.multiple_of(me_g * share, share), share)]
    for step in range(1, group):
        total = total + income[member(step)].astype(jnp.float32)
    reduced[...] = total.astype(jnp.bfloat16)
    gathered[me_g] = total.astype(jnp.bfloat16)
    gather = []
    for step in range(1, group):
        g = member(step)
        copy = pltpu.make_async_remote_copy(
            src_ref=reduced,
            dst_ref=gathered.at[me_g],
            send_sem=red_sem.at[2, step],
            recv_sem=red_sem.at[3, step],
            device_id=place(g),
            device_id_type=MESH,
        )
        copy.start()
        gather.append(copy)
    for copy in gather:
        copy.wait()

    scale = 1.0 / math.sqrt(width * height * gy_n * depth * gz_n)
    full = gathered[...].astype(jnp.float32).reshape(8 * rows, vec_n * rows) * scale
    along_x, along_z, phased, along_y = [
        full[slot * 2 * rows : (slot + 1) * 2 * rows] for slot in range(4)
    ]
    for slot in range(3):
        chosen = directions_ref[slot]
        out_ref[slot * 2 * rows : (slot + 1) * 2 * rows] = jnp.where(
            chosen == 0, along_x, jnp.where(chosen == 1, along_y, along_z)
        )
    out_ref[6 * rows :] = phased


def body(vectors, links, momentum, directions):
    rows, _, depth, height, lanes = vectors.shape
    gz_n = lax.axis_size("gz")
    gy_n = lax.axis_size("gy")
    vec_n = lax.axis_size("vec")
    group = gz_n * gy_n
    chunks = split_chunks(depth, 4)
    v = jnp.transpose(vectors, (2, 3, 1, 0, 4))
    packed = jnp.transpose(links, (0, 3, 4, 1, 2, 5)).reshape(3, depth, height, 9, lanes)

    share = 8 * rows // group
    bf16, f32 = jnp.bfloat16, jnp.float32
    pairs = vec_n // 2
    remote_count = 5 + chunks * (2 + 2 * (pairs - 1))
    vmem = pl.BlockSpec(memory_space=pltpu.VMEM)
    smem = pl.BlockSpec(memory_space=pltpu.SMEM)
    hbm = pl.BlockSpec(memory_space=pl.ANY)
    sizes = (gz_n, gy_n, vec_n, depth, height, rows, lanes // 2, chunks)
    out = pl.pallas_call(
        functools.partial(kernel, sizes),
        out_shape=jax.ShapeDtypeStruct((8 * rows, vec_n * rows), f32),
        in_specs=[smem, smem, hbm, vmem, hbm],
        out_specs=vmem,
        scratch_shapes=[
            pltpu.VMEM((depth + 2, height + 2, 3, rows, lanes), bf16),
            pltpu.VMEM((pairs, 2, depth, height, 3, rows, lanes), bf16),
            pltpu.VMEM((depth, 9, lanes), bf16),
            pltpu.VMEM((height, 9, lanes), bf16),
            pltpu.VMEM((2, depth, height, 32, lanes), f32),
            pltpu.VMEM((depth, height + 1, 32, lanes), f32),
            pltpu.VMEM((depth + 1, height, 32, lanes), f32),
            pltpu.VMEM((depth * height, lanes), f32),
            pltpu.VMEM((depth * height, lanes), f32),
            pltpu.VMEM((depth, height, 3, 8 * rows, lanes), bf16),
            pltpu.VMEM((8 * rows, vec_n * rows), f32),
            pltpu.VMEM((group, share, vec_n * rows), bf16),
            pltpu.VMEM((group, share, vec_n * rows), bf16),
            pltpu.VMEM((share, vec_n * rows), bf16),
            pltpu.VMEM((group, share, vec_n * rows), bf16),
            pltpu.SemaphoreType.DMA((2,)),
            pltpu.SemaphoreType.DMA((remote_count,)),
            pltpu.SemaphoreType.DMA((remote_count,)),
            pltpu.SemaphoreType.DMA((4, group)),
        ],
        compiler_params=pltpu.CompilerParams(
            collective_id=0, has_side_effects=True, vmem_limit_bytes=48 * 1024 * 1024
        ),
    )(momentum, directions, v, packed, packed)
    return out.reshape(4, 2, rows, vec_n * rows)


def solution(mesh):
    in_specs = (P("vec", None, "gz", "gy", None), P(None, None, None, "gz", "gy", None), P(), P())
    out_specs = P(None, None, "vec", None)
    return jax.shard_map(body, mesh=mesh, in_specs=in_specs, out_specs=out_specs, check_vma=False)
```

time: 62.9 us -> 46.6 us (0.74)
  Pallas kernels: 49.9 us -> 42.6 us
  between operations: 4.08 us -> 0.04 us
  other arithmetic: 3.88 us -> 0 us
  local copies, waits for them, and re-layouts: 4.73 us -> 3.74 us
    pallas_call x1, Pallas kernels: 49.9 us -> 42.6 us  [body(): pl.pallas_call(functools.partial(kernel, sizes), out_shape=jax.ShapeDtype...]
    unnamed x7, local copies, waits for them, and re-layouts: 1.69 us -> 3.7 us
    div x3 -> x0, other arithmetic: 1.88 us -> none  [the longest x1 0.66 us: body(): frac_z = (momentum[2] * z % extent_z).astype(jnp.float32) / extent_z]
    slice x5 -> x0, local copies, waits for them, and re-layouts: 1.66 us -> none  [the longest x1 0.61 us: body(): chosen = directions[slot]]
    reshape x4 -> x1, local copies, waits for them, and re-layouts: 1.28 us -> 0.03 us  [body(): jnp.transpose(links, (0, 3, 4, 1, 2, 5)).reshape(3, depth, height, 9, lanes)]
    mul x4 -> x0, other arithmetic: 0.92 us -> none  [the longest x1 0.86 us: body(): return jnp.stack(parts).astype(f32) * scale]
where the time goes in v2:
time: 46.6 us; the launch traced here: 46.4 us
  Pallas kernels  42.6 us (91%)
  local copies, waits for them, and re-layouts  3.74 us (8%)
    pallas_call x1, Pallas kernels, body(): pl.pallas_call(functools.partial(kernel, sizes), out_shape=jax.ShapeDtype...  42.6 us
    unnamed x7, local copies, waits for them, and re-layouts  3.7 us

profile of v2, /device:TPU:0, one launch (start us, length us, event | category | flops | bytes accessed | tf_op | source)
XLA Modules:
  0.0 46.4 jit_solution(12408698505504887871)
XLA Ops:
  0.0 0.9 %copy.8 = bf16[3,3,3,8,2,128]{5,3,2,1,4,0:T(8,128)(2,1)S(1)} copy(bf16[3,3,3,8,2,128]{5,4,3,2,1,0:T(2,128)(2,1)} %param.5) | data formatting | bytes 221184 | tf_op args[1]
  1.0 1.3 %copy.12 = bf16[64,3,8,2,128]{4,0,1,3,2:T(8,128)(2,1)S(1)} copy(bf16[64,3,8,2,128]{4,3,2,1,0:T(2,128)(2,1)} %param.4) | data formatting | bytes 1572864 | tf_op args[0]
  2.3 0.0 copy-start
  2.3 0.0 copy-start.1
  2.3 0.6 %copy-done = s32[3]{0:T(128)S(1)} copy-done((s32[3]{0:T(128)S(1)}, s32[3]{0:T(128)}, u32[]{:S(2)}) %copy-start) | copy-done | bytes 36
  3.0 0.0 copy-done.1
  3.0 42.6 %shard_map.46 = f32[512,256]{1,0:T(8,128)S(1)} custom-call(s32[3]{0:T(128)S(1)} %copy-done, s32[3]{0:T(128)S(1)} %copy-done.1, bf16[8,2,3,64,128]{4,3,2,1,0:T(8,128)(2,1)S(1)} %bitcast.7, bf16[3,8,2,9,128]{4,3,2,1,0:T(8,128)(2,1)S(1)} %copy.9.links_ref.links_far, bf16[3,8,2,9,128]{4,3,2,1,0:T(8,128)(2,1)S(1)} %copy.9.links_ref.links_far), custom_call_target="tpu_custom_call" | custom-call | tf_op jit(solution)/shard_map/pallas_call | solution.py:392
  45.6 0.8 %copy.14 = f32[4,2,64,256]{3,2,1,0:T(8,128)} copy(f32[4,2,64,256]{3,2,1,0:T(8,128)S(1)} %bitcast.8) | data formatting | bytes 1048576
  (1 shorter events, 0.0 us)
Async XLA Ops:
  2.3 0.7 %copy-start = (s32[3]{0:T(128)S(1)}, s32[3]{0:T(128)}, u32[]{:S(2)}) copy-start(s32[3]{0:T(128)} %momentum_ref.1) | copy-start | bytes 40
  2.3 0.7 %copy-start.1 = (s32[3]{0:T(128)S(1)}, s32[3]{0:T(128)}, u32[]{:S(2)}) copy-start(s32[3]{0:T(128)} %directions_ref.1) | copy-start | bytes 40

commit v3 on v2

--- a/solution.py
+++ b/solution.py
@@ -20,8 +20,8 @@
 
 def kernel(
     sizes,
-    momentum_ref,
-    directions_ref,
+    momentum_in,
+    directions_in,
     v_ref,
     links_ref,
     links_far,
@@ -37,6 +37,8 @@
     sin_ref,
     trans,
     acc,
+    momentum_ref,
+    directions_ref,
     outgo,
     income,
     reduced,
@@ -76,7 +78,11 @@
         pltpu.make_async_copy(v_ref, centre, local_sem.at[0]),
         pltpu.make_async_copy(v_ref, left.at[pair, side], local_sem.at[1]),
     ]
-    for copy in locals_:
+    scalars = [
+        pltpu.make_async_copy(momentum_in, momentum_ref, local_sem.at[2]),
+        pltpu.make_async_copy(directions_in, directions_ref, local_sem.at[3]),
+    ]
+    for copy in scalars + locals_:
         copy.start()
     pl.semaphore_wait(barrier, group - 1 + vec_n - 1)
 
@@ -143,6 +149,8 @@
     sign = jnp.where(low_half, 1.0, -1.0).astype(jnp.float32)
     tile = 32 if rows % 32 == 0 else rows
 
+    for copy in scalars:
+        copy.wait()
     site_shape = (depth * height, lanes)
     site = lax.broadcasted_iota(jnp.int32, site_shape, 0)
     x_at = lax.rem(lax.broadcasted_iota(jnp.int32, site_shape, 1), width)
@@ -299,6 +307,72 @@
     contract(pair, 0, 0, early, True)
     pl.loop(1, chunks)(lambda k: contract(pair, k, 0, early, False))
 
+    own_columns = pl.ds(pl.multiple_of(pair * 2 * rows, 2 * rows), 2 * rows)
+    stages = [
+        [(own_columns, 0, early)],
+        [
+            (
+                pl.ds(
+                    pl.multiple_of(lax.rem(pair + pairs - hop, pairs) * 2 * rows, 2 * rows),
+                    2 * rows,
+                ),
+                0,
+                8 * rows,
+            )
+            for hop in range(1, pairs)
+        ]
+        + [(own_columns, early, 8 * rows)],
+    ]
+
+    def exchange(stage, phase, step):
+        source = outgo[stage].at[member(step)] if phase == 0 else reduced[stage]
+        target = income[stage] if phase == 0 else gathered[stage]
+        return pltpu.make_async_remote_copy(
+            src_ref=source,
+            dst_ref=target.at[me_g],
+            send_sem=red_sem.at[stage, phase, 0, step],
+            recv_sem=red_sem.at[stage, phase, 1, step],
+            device_id=place(member(step)),
+            device_id_type=MESH,
+        )
+
+    def pieces(stage):
+        at = 0
+        for columns, lo, hi in stages[stage]:
+            share = (hi - lo) // group
+            yield columns, lo, share, at
+            at += share
+
+    def scatter_start(stage):
+        for columns, lo, share, at in pieces(stage):
+            for g in range(group):
+                outgo[stage][g, at : at + share] = acc[
+                    lo + g * share : lo + (g + 1) * share, columns
+                ].astype(jnp.bfloat16)
+        for step in range(1, group):
+            exchange(stage, 0, step).start()
+
+    def gather_start(stage):
+        for step in range(1, group):
+            exchange(stage, 0, step).wait()
+        total = outgo[stage][me_g].astype(jnp.float32)
+        for step in range(1, group):
+            total = total + income[stage][member(step)].astype(jnp.float32)
+        reduced[stage][...] = total.astype(jnp.bfloat16)
+        gathered[stage][me_g] = total.astype(jnp.bfloat16)
+        for step in range(1, group):
+            exchange(stage, 1, step).start()
+
+    def gather_finish(stage):
+        for step in range(1, group):
+            exchange(stage, 1, step).wait()
+        for columns, lo, share, at in pieces(stage):
+            for g in range(group):
+                acc[lo + g * share : lo + (g + 1) * share, columns] = gathered[stage][
+                    g, at : at + share
+                ].astype(jnp.float32)
+
+    scatter_start(0)
     rim_copy.wait()
 
     @pl.loop(0, depth)
@@ -315,51 +389,20 @@
                 index = k * (pairs - 1) + hop - 1
                 far[index].wait()
                 relay[index].start()
+        if k == chunks - 1:
+            gather_start(0)
         if k:
             for hop in range(1, pairs):
                 relay[(k - 1) * (pairs - 1) + hop - 1].wait()
                 contract(lax.rem(pair + pairs - hop, pairs), k - 1, 0, 8 * rows, k == 1)
 
-    share = 8 * rows // group
-    outgo[...] = acc[...].reshape(outgo.shape).astype(jnp.bfloat16)
-    scatter = []
-    for step in range(1, group):
-        g = member(step)
-        copy = pltpu.make_async_remote_copy(
-            src_ref=outgo.at[g],
-            dst_ref=income.at[me_g],
-            send_sem=red_sem.at[0, step],
-            recv_sem=red_sem.at[1, step],
-            device_id=place(g),
-            device_id_type=MESH,
-        )
-        copy.start()
-        scatter.append(copy)
-    for copy in scatter:
-        copy.wait()
-    total = acc[pl.ds(pl.multiple_of(me_g * share, share), share)]
-    for step in range(1, group):
-        total = total + income[member(step)].astype(jnp.float32)
-    reduced[...] = total.astype(jnp.bfloat16)
-    gathered[me_g] = total.astype(jnp.bfloat16)
-    gather = []
-    for step in range(1, group):
-        g = member(step)
-        copy = pltpu.make_async_remote_copy(
-            src_ref=reduced,
-            dst_ref=gathered.at[me_g],
-            send_sem=red_sem.at[2, step],
-            recv_sem=red_sem.at[3, step],
-            device_id=place(g),
-            device_id_type=MESH,
-        )
-        copy.start()
-        gather.append(copy)
-    for copy in gather:
-        copy.wait()
+    scatter_start(1)
+    gather_start(1)
+    gather_finish(0)
+    gather_finish(1)
 
     scale = 1.0 / math.sqrt(width * height * gy_n * depth * gz_n)
-    full = gathered[...].astype(jnp.float32).reshape(8 * rows, vec_n * rows) * scale
+    full = acc[...] * scale
     along_x, along_z, phased, along_y = [
         full[slot * 2 * rows : (slot + 1) * 2 * rows] for slot in range(4)
     ]
@@ -381,18 +424,17 @@
     v = jnp.transpose(vectors, (2, 3, 1, 0, 4))
     packed = jnp.transpose(links, (0, 3, 4, 1, 2, 5)).reshape(3, depth, height, 9, lanes)
 
-    share = 8 * rows // group
     bf16, f32 = jnp.bfloat16, jnp.float32
     pairs = vec_n // 2
+    shares = (6 * rows // group, (8 * (pairs - 1) + 2) * rows // group)
     remote_count = 5 + chunks * (2 + 2 * (pairs - 1))
     vmem = pl.BlockSpec(memory_space=pltpu.VMEM)
-    smem = pl.BlockSpec(memory_space=pltpu.SMEM)
     hbm = pl.BlockSpec(memory_space=pl.ANY)
     sizes = (gz_n, gy_n, vec_n, depth, height, rows, lanes // 2, chunks)
     out = pl.pallas_call(
         functools.partial(kernel, sizes),
         out_shape=jax.ShapeDtypeStruct((8 * rows, vec_n * rows), f32),
-        in_specs=[smem, smem, hbm, vmem, hbm],
+        in_specs=[hbm, hbm, hbm, vmem, hbm],
         out_specs=vmem,
         scratch_shapes=[
             pltpu.VMEM((depth + 2, height + 2, 3, rows, lanes), bf16),
@@ -406,14 +448,16 @@
             pltpu.VMEM((depth * height, lanes), f32),
             pltpu.VMEM((depth, height, 3, 8 * rows, lanes), bf16),
             pltpu.VMEM((8 * rows, vec_n * rows), f32),
-            pltpu.VMEM((group, share, vec_n * rows), bf16),
-            pltpu.VMEM((group, share, vec_n * rows), bf16),
-            pltpu.VMEM((share, vec_n * rows), bf16),
-            pltpu.VMEM((group, share, vec_n * rows), bf16),
-            pltpu.SemaphoreType.DMA((2,)),
+            pltpu.SMEM((3,), jnp.int32),
+            pltpu.SMEM((3,), jnp.int32),
+            [pltpu.VMEM((group, share, 2 * rows), bf16) for share in shares],
+            [pltpu.VMEM((group, share, 2 * rows), bf16) for share in shares],
+            [pltpu.VMEM((share, 2 * rows), bf16) for share in shares],
+            [pltpu.VMEM((group, share, 2 * rows), bf16) for share in shares],
+            pltpu.SemaphoreType.DMA((4,)),
             pltpu.SemaphoreType.DMA((remote_count,)),
             pltpu.SemaphoreType.DMA((remote_count,)),
-            pltpu.SemaphoreType.DMA((4, group)),
+            pltpu.SemaphoreType.DMA((2, 2, 2, group)),
         ],
         compiler_params=pltpu.CompilerParams(
             collective_id=0, has_side_effects=True, vmem_limit_bytes=48 * 1024 * 1024

time: 46.6 us -> 44.5 us (0.955)
  Pallas kernels: 42.6 us -> 40.5 us
    pallas_call x1, Pallas kernels: 42.6 us -> 40.5 us  [body(): pl.pallas_call(functools.partial(kernel, sizes), out_shape=jax.ShapeDtype...]
where the time goes in v3:
time: 44.5 us; the launch traced here: 44.3 us
  Pallas kernels  40.5 us (91%)
  local copies, waits for them, and re-layouts  3.74 us (8%)
    pallas_call x1, Pallas kernels, body(): pl.pallas_call(functools.partial(kernel, sizes), out_shape=jax.ShapeDtype...  40.5 us
    unnamed x7, local copies, waits for them, and re-layouts  3.7 us

profile of v3, /device:TPU:0, one launch (start us, length us, event | category | flops | bytes accessed | tf_op | source)
XLA Modules:
  0.0 44.3 jit_solution(17164061032039712527)
XLA Ops:
  0.0 0.9 %copy.8 = bf16[3,3,3,8,2,128]{5,3,2,1,4,0:T(8,128)(2,1)S(1)} copy(bf16[3,3,3,8,2,128]{5,4,3,2,1,0:T(2,128)(2,1)} %param.5) | data formatting | bytes 221184 | tf_op args[1]
  1.0 1.3 %copy.12 = bf16[64,3,8,2,128]{4,0,1,3,2:T(8,128)(2,1)S(1)} copy(bf16[64,3,8,2,128]{4,3,2,1,0:T(2,128)(2,1)} %param.4) | data formatting | bytes 1572864 | tf_op args[0]
  2.3 0.0 copy-start
  2.3 0.0 copy-start.1
  2.3 0.6 %copy-done = s32[3]{0:T(128)S(1)} copy-done((s32[3]{0:T(128)S(1)}, s32[3]{0:T(128)}, u32[]{:S(2)}) %copy-start) | copy-done | bytes 36
  3.0 0.0 copy-done.1
  3.0 40.5 %shard_map.46 = f32[512,256]{1,0:T(8,128)S(1)} custom-call(s32[3]{0:T(128)S(1)} %copy-done, s32[3]{0:T(128)S(1)} %copy-done.1, bf16[8,2,3,64,128]{4,3,2,1,0:T(8,128)(2,1)S(1)} %bitcast.7, bf16[3,8,2,9,128]{4,3,2,1,0:T(8,128)(2,1)S(1)} %copy.9.links_ref.links_far, bf16[3,8,2,9,128]{4,3,2,1,0:T(8,128)(2,1)S(1)} %copy.9.links_ref.links_far), custom_call_target="tpu_custom_call" | custom-call | tf_op jit(solution)/shard_map/pallas_call | solution.py:434
  43.5 0.8 %copy.14 = f32[4,2,64,256]{3,2,1,0:T(8,128)} copy(f32[4,2,64,256]{3,2,1,0:T(8,128)S(1)} %bitcast.8) | data formatting | bytes 1048576
  (1 shorter events, 0.0 us)
Async XLA Ops:
  2.3 0.7 %copy-start = (s32[3]{0:T(128)S(1)}, s32[3]{0:T(128)}, u32[]{:S(2)}) copy-start(s32[3]{0:T(128)} %momentum_in.1) | copy-start | bytes 40
  2.3 0.7 %copy-start.1 = (s32[3]{0:T(128)S(1)}, s32[3]{0:T(128)}, u32[]{:S(2)}) copy-start(s32[3]{0:T(128)} %directions_in.1) | copy-start | bytes 40

commit v4 on v3

--- a/solution.py
+++ b/solution.py
@@ -381,14 +381,14 @@
 
     for k in range(chunks + 1):
         if k < chunks:
+            for hop in range(1, pairs):
+                index = k * (pairs - 1) + hop - 1
+                far[index].wait()
+                relay[index].start()
             for copy in y_copies[k]:
                 copy.wait()
             pl.loop(k * span, (k + 1) * span)(pass_y)
             contract(pair, k, early, 8 * rows, k == 0)
-            for hop in range(1, pairs):
-                index = k * (pairs - 1) + hop - 1
-                far[index].wait()
-                relay[index].start()
         if k == chunks - 1:
             gather_start(0)
         if k:
@@ -420,7 +420,7 @@
     gy_n = lax.axis_size("gy")
     vec_n = lax.axis_size("vec")
     group = gz_n * gy_n
-    chunks = split_chunks(depth, 4)
+    chunks = split_chunks(depth, 8)
     v = jnp.transpose(vectors, (2, 3, 1, 0, 4))
     packed = jnp.transpose(links, (0, 3, 4, 1, 2, 5)).reshape(3, depth, height, 9, lanes)
 

time: 44.5 us -> 46.1 us (1.036)
  Pallas kernels: 40.5 us -> 42.2 us
    pallas_call x1, Pallas kernels: 40.5 us -> 42.2 us  [body(): pl.pallas_call(functools.partial(kernel, sizes), out_shape=jax.ShapeDtype...]
where the time goes in v4:
time: 46.1 us; the launch traced here: 46 us
  Pallas kernels  42.2 us (92%)
  local copies, waits for them, and re-layouts  3.74 us (8%)
    pallas_call x1, Pallas kernels, body(): pl.pallas_call(functools.partial(kernel, sizes), out_shape=jax.ShapeDtype...  42.2 us
    unnamed x7, local copies, waits for them, and re-layouts  3.7 us

profile of v4, /device:TPU:0, one launch (start us, length us, event | category | flops | bytes accessed | tf_op | source)
XLA Modules:
  0.0 46.0 jit_solution(10901745451315719574)
XLA Ops:
  0.0 0.9 %copy.8 = bf16[3,3,3,8,2,128]{5,3,2,1,4,0:T(8,128)(2,1)S(1)} copy(bf16[3,3,3,8,2,128]{5,4,3,2,1,0:T(2,128)(2,1)} %param.5) | data formatting | bytes 221184 | tf_op args[1]
  1.0 1.3 %copy.12 = bf16[64,3,8,2,128]{4,0,1,3,2:T(8,128)(2,1)S(1)} copy(bf16[64,3,8,2,128]{4,3,2,1,0:T(2,128)(2,1)} %param.4) | data formatting | bytes 1572864 | tf_op args[0]
  2.3 0.0 copy-start
  2.3 0.0 copy-start.1
  2.3 0.6 %copy-done = s32[3]{0:T(128)S(1)} copy-done((s32[3]{0:T(128)S(1)}, s32[3]{0:T(128)}, u32[]{:S(2)}) %copy-start) | copy-done | bytes 36
  3.0 0.0 copy-done.1
  3.0 42.2 %shard_map.46 = f32[512,256]{1,0:T(8,128)S(1)} custom-call(s32[3]{0:T(128)S(1)} %copy-done, s32[3]{0:T(128)S(1)} %copy-done.1, bf16[8,2,3,64,128]{4,3,2,1,0:T(8,128)(2,1)S(1)} %bitcast.7, bf16[3,8,2,9,128]{4,3,2,1,0:T(8,128)(2,1)S(1)} %copy.9.links_ref.links_far, bf16[3,8,2,9,128]{4,3,2,1,0:T(8,128)(2,1)S(1)} %copy.9.links_ref.links_far), custom_call_target="tpu_custom_call" | custom-call | tf_op jit(solution)/shard_map/pallas_call | solution.py:434
  45.2 0.8 %copy.14 = f32[4,2,64,256]{3,2,1,0:T(8,128)} copy(f32[4,2,64,256]{3,2,1,0:T(8,128)S(1)} %bitcast.8) | data formatting | bytes 1048576
  (1 shorter events, 0.0 us)
Async XLA Ops:
  2.3 0.7 %copy-start = (s32[3]{0:T(128)S(1)}, s32[3]{0:T(128)}, u32[]{:S(2)}) copy-start(s32[3]{0:T(128)} %momentum_in.1) | copy-start | bytes 40
  2.3 0.7 %copy-start.1 = (s32[3]{0:T(128)S(1)}, s32[3]{0:T(128)}, u32[]{:S(2)}) copy-start(s32[3]{0:T(128)} %directions_in.1) | copy-start | bytes 40

commit v5 on v4

--- a/solution.py
+++ b/solution.py
@@ -420,7 +420,7 @@
     gy_n = lax.axis_size("gy")
     vec_n = lax.axis_size("vec")
     group = gz_n * gy_n
-    chunks = split_chunks(depth, 8)
+    chunks = split_chunks(depth, 4)
     v = jnp.transpose(vectors, (2, 3, 1, 0, 4))
     packed = jnp.transpose(links, (0, 3, 4, 1, 2, 5)).reshape(3, depth, height, 9, lanes)
 

time: 46.1 us -> 43.7 us (0.948)
  Pallas kernels: 42.2 us -> 39.8 us
    pallas_call x1, Pallas kernels: 42.2 us -> 39.8 us  [body(): pl.pallas_call(functools.partial(kernel, sizes), out_shape=jax.ShapeDtype...]
where the time goes in v5:
time: 43.7 us; the launch traced here: 43.6 us
  Pallas kernels  39.8 us (91%)
  local copies, waits for them, and re-layouts  3.74 us (9%)
    pallas_call x1, Pallas kernels, body(): pl.pallas_call(functools.partial(kernel, sizes), out_shape=jax.ShapeDtype...  39.8 us
    unnamed x7, local copies, waits for them, and re-layouts  3.7 us

profile of v5, /device:TPU:0, one launch (start us, length us, event | category | flops | bytes accessed | tf_op | source)
XLA Modules:
  0.0 43.6 jit_solution(17235026366733200226)
XLA Ops:
  0.0 0.9 %copy.8 = bf16[3,3,3,8,2,128]{5,3,2,1,4,0:T(8,128)(2,1)S(1)} copy(bf16[3,3,3,8,2,128]{5,4,3,2,1,0:T(2,128)(2,1)} %param.5) | data formatting | bytes 221184 | tf_op args[1]
  1.0 1.3 %copy.12 = bf16[64,3,8,2,128]{4,0,1,3,2:T(8,128)(2,1)S(1)} copy(bf16[64,3,8,2,128]{4,3,2,1,0:T(2,128)(2,1)} %param.4) | data formatting | bytes 1572864 | tf_op args[0]
  2.3 0.0 copy-start
  2.3 0.0 copy-start.1
  2.3 0.6 %copy-done = s32[3]{0:T(128)S(1)} copy-done((s32[3]{0:T(128)S(1)}, s32[3]{0:T(128)}, u32[]{:S(2)}) %copy-start) | copy-done | bytes 36
  3.0 0.0 copy-done.1
  3.0 39.8 %shard_map.46 = f32[512,256]{1,0:T(8,128)S(1)} custom-call(s32[3]{0:T(128)S(1)} %copy-done, s32[3]{0:T(128)S(1)} %copy-done.1, bf16[8,2,3,64,128]{4,3,2,1,0:T(8,128)(2,1)S(1)} %bitcast.7, bf16[3,8,2,9,128]{4,3,2,1,0:T(8,128)(2,1)S(1)} %copy.9.links_ref.links_far, bf16[3,8,2,9,128]{4,3,2,1,0:T(8,128)(2,1)S(1)} %copy.9.links_ref.links_far), custom_call_target="tpu_custom_call" | custom-call | tf_op jit(solution)/shard_map/pallas_call | solution.py:434
  42.8 0.8 %copy.14 = f32[4,2,64,256]{3,2,1,0:T(8,128)} copy(f32[4,2,64,256]{3,2,1,0:T(8,128)S(1)} %bitcast.8) | data formatting | bytes 1048576
  (1 shorter events, 0.0 us)
Async XLA Ops:
  2.3 0.7 %copy-start = (s32[3]{0:T(128)S(1)}, s32[3]{0:T(128)}, u32[]{:S(2)}) copy-start(s32[3]{0:T(128)} %momentum_in.1) | copy-start | bytes 40
  2.3 0.7 %copy-start.1 = (s32[3]{0:T(128)S(1)}, s32[3]{0:T(128)}, u32[]{:S(2)}) copy-start(s32[3]{0:T(128)} %directions_in.1) | copy-start | bytes 40
